TPU v7x, 32 devices: a whole 2x2x4 slice. The times are simulated.
32 devices in a mesh: row: 4 (over y, x), col: 8 (over z, core).
Axes of the slice: x: 2, y: 2, z: 4, core: 2. Of those that a mesh axis runs over, the one named last changes fastest.
Arguments:
- activations: bfloat16 [8192, 1024], P(('row', 'col')), may hold values from -6 to 6
- out_grads: bfloat16 [28672, 1024], P(('row', 'col')), may hold values from -0.0059814453 to 0.0059814453
- accumulated: float32 [28672, 8192], P(('row', 'col')), may hold values from -0.18 to 0.18
- seed_basis: float32 [8192, 512], P('row'), may hold values from -6 to 6
- moment_first: float32 [28672, 512], P(('row', 'col')), may hold values from -0.6 to 0.6
- moment_second: float32 [28672, 512], P(('row', 'col')), may hold values from 0.001 to 0.1
Outputs:
- basis: bfloat16 [8192, 512], P(('row', 'col'))
- first_next: float32 [28672, 512], P(('row', 'col'))
- second_next: float32 [28672, 512], P(('row', 'col'))
- lifted: float32 [28672, 8192], P(('row', 'col'))
All inputs are finite; a program needn't handle non-finite values.
Results may differ from a plain program's by a relative error of at most 0.0029.
Values may be sent and summed in bfloat16 or wider, within the bound.
A program may use at most 192 MiB of HBM per device.

v0:
```python
import jax
import jax.numpy as jnp
from jax import lax
from jax.sharding import PartitionSpec as P

beta_first = 0.9
beta_second = 0.99
correct_first = 1.0 - 0.9**10
correct_second = 1.0 - 0.99**10
epsilon_value = 1e-08
lift_scale = 8.0

every = ("row", "col")
highest = lax.Precision.HIGHEST
high = lax.Precision.HIGH


def mul(left, right, dims, precision=None):
    return lax.dot_general(
        left, right, (dims, ((), ())), precision=precision, preferred_element_type=jnp.float32
    )


rows_cols = ((1,), (0,))
rows_rows = ((0,), (0,))
cols_cols = ((1,), (1,))


def solve_lower(gram_matrix, right):
    rank = gram_matrix.shape[0]
    step = 128 if rank % 128 == 0 else rank
    count = rank // step
    cut = lambda n: slice(n * step, (n + 1) * step)
    trailing = {
        (i, j): gram_matrix[cut(i), cut(j)] for i in range(count) for j in range(i + 1)
    }
    rests = [right[cut(i)] for i in range(count)]
    solved = []
    for j in range(count):
        factor = lax.linalg.cholesky(trailing[j, j], symmetrize_input=False)
        inverse = jax.scipy.linalg.solve_triangular(
            factor, jnp.eye(step, dtype=jnp.float32), lower=True
        )
        panel = {
            i: mul(trailing[i, j], inverse, cols_cols, highest) for i in range(j + 1, count)
        }
        solved.append(mul(inverse, rests[j], rows_cols, highest))
        for i in range(j + 1, count):
            rests[i] = rests[i] - mul(panel[i], solved[j], rows_cols, highest)
            for k in range(j + 1, i + 1):
                trailing[i, k] = trailing[i, k] - mul(panel[i], panel[k], cols_cols, highest)
    return jnp.concatenate(solved, axis=0)


def body(activations, out_grads, accumulated, seed_basis, moment_first, moment_second):
    share_rows = activations.shape[0]
    acts = activations.astype(jnp.float32)
    grads = out_grads.astype(jnp.float32)
    own_seed = lax.dynamic_slice_in_dim(
        seed_basis, lax.axis_index("col") * share_rows, share_rows, 0
    )
    full_seed = lax.all_gather(own_seed, every, axis=0, tiled=True)
    seed_tokens = lax.psum(mul(acts, own_seed, rows_rows, highest), every)
    image_rows = mul(accumulated, full_seed, rows_cols, high) + mul(
        grads, seed_tokens, rows_cols, high
    )
    image_tokens = lax.psum(mul(grads, image_rows, rows_rows, high), every)
    power_part = mul(accumulated, image_rows, rows_rows, high)
    power_rows = lax.psum_scatter(
        power_part, every, scatter_dimension=0, tiled=True
    ) + mul(acts, image_tokens, rows_cols, highest)
    gram_matrix = lax.psum(mul(power_rows, power_rows, rows_rows, highest), every)
    gram_matrix, held_acts = lax.optimization_barrier((gram_matrix, activations))
    full_acts = lax.all_gather(held_acts, every, axis=0, tiled=True)
    solved = solve_lower(gram_matrix, power_rows.T)
    basis_rows = solved.T.astype(jnp.bfloat16)
    sent_rows, full_acts = lax.optimization_barrier((basis_rows, full_acts))
    full_basis = lax.all_gather(sent_rows, every, axis=0, tiled=True)
    basis_tokens = mul(full_acts, full_basis, rows_rows)
    projected = mul(accumulated.astype(jnp.bfloat16), full_basis, rows_cols) + mul(
        grads, basis_tokens, rows_cols, high
    )
    first_next = beta_first * moment_first + (1.0 - beta_first) * projected
    second_next = beta_second * moment_second + (1.0 - beta_second) * projected * projected
    direction = (
        first_next / correct_first / (jnp.sqrt(second_next / correct_second) + epsilon_value)
    )
    lifted = lift_scale * mul(direction.astype(jnp.bfloat16), full_basis, cols_cols)
    return (basis_rows, first_next, second_next, lifted)


def solution(mesh):
    in_specs = (
        P(("row", "col"), None),
        P(("row", "col"), None),
        P(("row", "col"), None),
        P("row", None),
        P(("row", "col"), None),
        P(("row", "col"), None),
    )
    out_specs = (
        P(("row", "col"), None),
        P(("row", "col"), None),
        P(("row", "col"), None),
        P(("row", "col"), None),
    )
    return jax.shard_map(body, mesh=mesh, in_specs=in_specs, out_specs=out_specs, check_vma=False)
```

profile of v0, /device:TPU:25, one launch (start us, length us, event | category | flops | bytes accessed | tf_op | source)
XLA Modules:
  0.0 1060.8 jit_solution(17381407855342865529)
XLA Ops:
  8.4 3.6 convolution_bitcast_fusion.2
  12.9 133.6 %all-reduce.4.cloned.1.call-done = f32[1024,512]{0,1:T(8,128)} async-done(((f32[1024,512]{0,1:T(8,128)}), f32[1024,512]{0,1:T(8,128)}) %all-reduce.4.cloned.1.call-update) | async-done | bytes 2097168 | tf_op jit(solution)/shard_map/psum | solution.py:63
  146.5 5.2 fusion.38
  151.6 113.3 %all-gather.4.cloned.1.call-done = f32[8192,512]{1,0:T(8,128)} async-done(((f32[256,512]{1,0:T(8,128)}), f32[8192,512]{1,0:T(8,128)}) %all-gather.4.cloned.1.call-update) | async-done | bytes 16777232 | tf_op jit(solution)/shard_map/all_gather | solution.py:62
  264.9 58.7 %convolution_add_fusion = f32[512,896]{1,0:T(8,128)S(1)} fusion(f32[512,896]{1,0:T(8,128)} %fusion.38, f32[8192,512]{1,0:T(8,128)} %all-gather.4.cloned.1.call-done, f32[896,8192]{1,0:T(8,128)} %param.11), kind=kOutput, calls=%fused_computation.11 | convolution fusion | flops 22549037056 | bytes 49807360 | tf_op jit(solution)/shard_map/dot_general | solution.py:19
  324.9 3.6 convolution_bitcast_fusion.1
  328.6 33.1 %convolution_bitcast_fusion = f32[8192,512]{0,1:T(8,128)} fusion(f32[512,896]{1,0:T(8,128)} %copy-done.3, f32[896,8192]{1,0:T(8,128)} %param.11), kind=kOutput, calls=%fused_computation.3 | convolution fusion | flops 22548578304 | bytes 47972352 | tf_op jit(solution)/shard_map/dot_general | solution.py:19
  361.8 98.1 %all-reduce.6.cloned.1.call-done = f32[1024,512]{0,1:T(8,128)} async-done(((f32[1024,512]{0,1:T(8,128)}), f32[1024,512]{0,1:T(8,128)}) %all-reduce.6.cloned.1.call-update) | async-done | bytes 2097168 | tf_op jit(solution)/shard_map/psum | solution.py:67
  459.9 187.6 %reduce-scatter.2.cloned.1.call-done = f32[256,512]{0,1:T(8,128)} async-done(((f32[8192,512]{0,1:T(8,128)}), f32[256,512]{0,1:T(8,128)}) %reduce-scatter.2.cloned.1.call-update) | async-done | bytes 524304 | tf_op jit(solution)/shard_map/reduce_scatter | solution.py:69
  652.4 129.8 %all-reduce.8.cloned.1.call-done = f32[512,512]{1,0:T(8,128)} async-done(((f32[512,512]{1,0:T(8,128)}), f32[512,512]{1,0:T(8,128)}) %all-reduce.8.cloned.1.call-update) | async-done | bytes 1048592 | tf_op jit(solution)/shard_map/psum | solution.py:72
  783.3 11.7 %custom-call.12 = f32[128,128]{1,0:T(8,128)S(1)} custom-call(f32[128,128]{1,0:T(8,128)S(1)} %slice.48), custom_call_target="Cholesky" | custom-call | tf_op jit(solution)/shard_map/cholesky/custom-call.1 | solution.py:40
  796.4 9.8 custom-call.13
  808.7 11.7 %custom-call.14 = f32[128,128]{1,0:T(8,128)S(1)} custom-call(f32[128,128]{1,0:T(8,128)S(1)} %convolution_subtract_fusion.15), custom_call_target="Cholesky" | custom-call | tf_op jit(solution)/shard_map/cholesky/custom-call.1 | solution.py:40
  821.8 10.2 custom-call.15
  836.1 11.7 %custom-call.16 = f32[128,128]{1,0:T(8,128)S(1)} custom-call(f32[128,128]{1,0:T(8,128)S(1)} %convolution_subtract_fusion.12), custom_call_target="Cholesky" | custom-call | tf_op jit(solution)/shard_map/cholesky/custom-call.1 | solution.py:40
  849.2 9.8 custom-call.17
  865.1 11.9 %custom-call.18 = f32[128,128]{1,0:T(8,128)S(1)} custom-call(f32[128,128]{1,0:T(8,128)S(1)} %convolution_subtract_fusion.6), custom_call_target="Cholesky" | custom-call | tf_op jit(solution)/shard_map/cholesky/custom-call.1 | solution.py:40
  878.3 9.8 custom-call.19
  891.8 8.4 all-gather.6.cloned.1.call-done
  906.6 84.5 %all-gather.8.cloned.1.call-done = bf16[8192,512]{0,1:T(8,128)(2,1)} async-done(((bf16[256,512]{0,1:T(8,128)(2,1)}), bf16[8192,512]{0,1:T(8,128)(2,1)}) %all-gather.8.cloned.1.call-update) | async-done | bytes 8388624 | tf_op jit(solution)/shard_map/all_gather | solution.py:78
  991.1 17.6 %fusion = f32[512,896]{1,0:T(8,128)} fusion(bf16[8192,512]{0,1:T(8,128)(2,1)} %all-gather.8.cloned.1.call-done, f32[896,8192]{1,0:T(8,128)} %param.11), kind=kOutput, calls=%fused_computation.1 | convolution fusion | flops 7523532800 | bytes 39583744 | tf_op jit(solution)/shard_map/dot_general | solution.py:19
  1008.7 14.4 %fusion.43 = f32[1024,512]{1,0:T(8,128)S(1)} fusion(bf16[8192,1024]{1,0:T(8,128)(2,1)} %all-gather.6.cloned.1.call-done, bf16[8192,512]{0,1:T(8,128)(2,1)} %all-gather.8.cloned.1.call-done), kind=kOutput, calls=%fused_computation.86 | convolution fusion | flops 8589934592 | bytes 27262976 | tf_op jit(solution)/shard_map/dot_general | solution.py:19
  1023.1 6.7 fusion.2
  1035.3 18.4 %convolution_multiply_fusion = f32[896,8192]{1,0:T(8,128)} fusion(bf16[8192,512]{0,1:T(8,128)(2,1)} %all-gather.8.cloned.1.call-done, f32[896,512]{0,1:T(8,128)} %get-tuple-element.18, f32[896,512]{0,1:T(8,128)} %get-tuple-element.19), kind=kOutput, calls=%fused_computation | convolution fusion | flops 7525826560 | bytes 41418752 | tf_op jit(solution)/shard_map/dot_general | solution.py:19
  (82 shorter events, 42.8 us)
Async XLA Ops:
  7.2 139.3 %copy-start = (bf16[896,1024]{1,0:T(8,128)(2,1)S(1)}, bf16[896,1024]{1,0:T(8,128)(2,1)}, u32[]{:S(2)}) copy-start(bf16[896,1024]{1,0:T(8,128)(2,1)} %param.10) | copy-start | bytes 5505028
  7.2 139.3 %all-reduce.4.cloned.1.call-start = ((), (), s32[]{:S(2)}) async-start(), calls=%async_computation.2 | async-start | bytes 4194304 | tf_op jit(solution)/shard_map/psum | solution.py:63
  8.4 3.6 copy-start.5
  12.1 252.9 %all-gather.4.cloned.1.call-start = ((), (), s32[]{:S(2)}) async-start(), calls=%async_computation.1 | async-start | bytes 17301504 | tf_op jit(solution)/shard_map/all_gather | solution.py:62
  12.8 447.1 %all-reduce.6.cloned.1.call-start = ((), (), s32[]{:S(2)}) async-start(), calls=%async_computation.4 | async-start | bytes 4194304 | tf_op jit(solution)/shard_map/psum | solution.py:67
  323.7 1.2 copy-start.3
  328.6 319.0 %reduce-scatter.2.cloned.1.call-start = ((), (), s32[]{:S(2)}) async-start(), calls=%async_computation.3 | async-start | bytes 17301504 | tf_op jit(solution)/shard_map/reduce_scatter | solution.py:69
  361.7 285.8 %copy-start.4 = (bf16[256,1024]{1,0:T(8,128)(2,1)S(1)}, bf16[256,1024]{1,0:T(8,128)(2,1)}, u32[]{:S(2)}) copy-start(bf16[256,1024]{1,0:T(8,128)(2,1)} %param.9) | copy-start | bytes 1572868
  361.7 420.5 %all-reduce.8.cloned.1.call-start = ((), (), s32[]{:S(2)}) async-start(), calls=%async_computation.5 | async-start | bytes 2097152 | tf_op jit(solution)/shard_map/psum | solution.py:72
  652.3 247.9 %all-gather.6.cloned.1.call-start = ((), (), s32[]{:S(2)}) async-start(), calls=%async_computation.6 | async-start | bytes 17301504 | tf_op jit(solution)/shard_map/all_gather | solution.py:74
  782.3 208.9 %all-gather.8.cloned.1.call-start = ((), (), s32[]{:S(2)}) async-start(), calls=%async_computation.7 | async-start | bytes 8650752 | tf_op jit(solution)/shard_map/all_gather | solution.py:78
  903.0 2.8 copy-start.6
  1008.7 14.4 %copy-start.1 = (f32[896,512]{0,1:T(8,128)S(1)}, f32[896,512]{0,1:T(8,128)}, u32[]{:S(2)}) copy-start(f32[896,512]{0,1:T(8,128)} %copy.10) | copy-start | bytes 5505028
  1008.7 14.4 %copy-start.2 = (f32[896,512]{0,1:T(8,128)S(1)}, f32[896,512]{0,1:T(8,128)}, u32[]{:S(2)}) copy-start(f32[896,512]{0,1:T(8,128)} %copy.11) | copy-start | bytes 5505028
  1008.7 14.4 %copy-start.7 = (f32[512,896]{1,0:T(8,128)S(1)}, f32[512,896]{1,0:T(8,128)}, u32[]{:S(2)}) copy-start(f32[512,896]{1,0:T(8,128)} %fusion) | copy-start | bytes 5505028
Sparse Core Ops, SparseCore 0:
  13.9 132.5 all-reduce.3
  150.0 114.8 all-gather.3
  328.7 131.1 all-reduce.5
  462.6 184.8 reduce-scatter.1
  653.1 129.0 all-reduce.7
  785.1 115.0 all-gather.5
  903.7 87.3 all-gather.7
where the time goes:
time: 1070 us; the launch traced here: 1060 us
  waiting for transfers between devices  756 us (71%)
  matrix products  182 us (17%)
  other arithmetic  92.7 us (9%)
  local copies, waits for them, and re-layouts  15.1 us (1%)
  between operations  14.6 us (1%)
    reduce_scatter x1, waiting for transfers between devices, body(): lax.psum_scatter(power_part, every, scatter_dimension=0, tiled=True)  188 us
    dot_general x37, matrix products, mul(): lax.dot_general(left, right, (dims, ((), ())), precision=precision, prefe...  181 us
    psum x1, waiting for transfers between devices, body(): seed_tokens = lax.psum(mul(acts, own_seed, rows_rows, highest), every)  134 us
    psum x1, waiting for transfers between devices, body(): lax.psum(mul(power_rows, power_rows, rows_rows, highest), every)  130 us
    all_gather x1, waiting for transfers between devices, body(): full_seed = lax.all_gather(own_seed, every, axis=0, tiled=True)  113 us
    psum x1, waiting for transfers between devices, body(): image_tokens = lax.psum(mul(grads, image_rows, rows_rows, high), every)  98.1 us
    all_gather x1, waiting for transfers between devices, body(): full_basis = lax.all_gather(sent_rows, every, axis=0, tiled=True)  84.5 us
    another operation x12, other arithmetic, solve_lower(): factor = lax.linalg.cholesky(trailing[j, j], symmetrize_input=False)  49.7 us
  transfers between devices with their start and end apart: 7, of which 7 were waited for; matrix products, arithmetic and copies ran while one was open for 14% of the time, Pallas kernels for 0%

commit v1 on v0

--- a/solution.py
+++ b/solution.py
@@ -1,6 +1,10 @@
+import functools
+
 import jax
 import jax.numpy as jnp
 from jax import lax
+from jax.experimental import pallas as pl
+from jax.experimental.pallas import tpu as pltpu
 from jax.sharding import PartitionSpec as P
 
 beta_first = 0.9
@@ -13,6 +17,13 @@
 every = ("row", "col")
 highest = lax.Precision.HIGHEST
 high = lax.Precision.HIGH
+bf16 = jnp.bfloat16
+f32 = jnp.float32
+MESH = pl.DeviceIdType.MESH
+ANY = pl.BlockSpec(memory_space=pl.ANY)
+VMEM = pl.BlockSpec(memory_space=pltpu.VMEM)
+DMA = pltpu.SemaphoreType.DMA
+vmem_bytes = 63 * 2**20
 
 
 def mul(left, right, dims, precision=None):
@@ -24,6 +35,382 @@
 rows_cols = ((1,), (0,))
 rows_rows = ((0,), (0,))
 cols_cols = ((1,), (1,))
+
+
+def split(value):
+    upper = value.astype(bf16)
+    return upper, (value - upper.astype(f32)).astype(bf16)
+
+
+class Grid:
+    def __init__(self, rows, cols):
+        self.rows, self.chips = rows, cols // 2
+        self.stages = rows.bit_length() - 1
+        self.r = lax.axis_index("row")
+        c = lax.axis_index("col")
+        self.z, self.k = c // 2, c % 2
+        self.c = c
+        self.partner = (self.r, self.z * 2 + 1 - self.k)
+
+    def flip(self, bit):
+        return self.r + bit * (1 - 2 * ((self.r // bit) % 2))
+
+    def peer_row(self, s):
+        low, high_bit = 2**s, 2 ** (self.stages - 1 - s)
+        return (1 - self.k) * self.flip(low) + self.k * self.flip(high_bit)
+
+    def peer(self, s):
+        return (self.peer_row(s), self.c)
+
+    def count(self, s):
+        return 2 ** (self.stages - 1 - s)
+
+    def block(self, s, j, base):
+        n = self.count(s)
+        first = base % 2 ** (s + 1) + j * 2 ** (s + 1)
+        second = (base // n) * n + j
+        return (1 - self.k) * first + self.k * second
+
+    def chip(self, w):
+        n = self.chips
+        return (self.z + 1 + w) % n, (self.z + n - 1 - w) % n
+
+    def chip_device(self, z):
+        return (self.r, z * 2 + self.k)
+
+    def greet(self):
+        barrier = pltpu.get_barrier_semaphore()
+        peers = [self.partner]
+        peers += [self.peer(s) for s in range(self.stages)]
+        peers += [self.chip_device(self.chip(w)[0]) for w in range(self.chips - 1)]
+        for peer in peers:
+            pl.semaphore_signal(barrier, inc=1, device_id=peer, device_id_type=MESH)
+        pl.semaphore_wait(barrier, len(peers))
+
+
+def remote(source, target, send, recv, device):
+    return pltpu.make_async_remote_copy(
+        src_ref=source, dst_ref=target, send_sem=send, recv_sem=recv,
+        device_id=device, device_id_type=MESH,
+    )
+
+
+class AllReduce:
+    def __init__(self, grid, part, full, half_in, stage_in, chip_in, send, recv):
+        self.g, self.part, self.full = grid, part, full
+        self.half_in, self.stage_in, self.chip_in = half_in, stage_in, chip_in
+        self.send, self.recv = send, recv
+        self.half = part.shape[0] // 2
+        self.chunk = self.half // grid.rows
+        self.unit = self.chunk // grid.chips
+        self.pending = []
+        self.used = 0
+        self.phases = (
+            [self.pair_out]
+            + [functools.partial(self.halve, s) for s in range(grid.stages)]
+            + [self.chips_out, self.chips_back]
+            + [functools.partial(self.double, s) for s in reversed(range(grid.stages))]
+            + [self.pair_back, self.finish]
+        )
+        self.arrived = []
+
+    @staticmethod
+    def scratch(rows, width, grid_rows, chips):
+        half = rows // 2
+        chunk = half // grid_rows
+        stages = grid_rows.bit_length() - 1
+        copies = 2 + 2 * (grid_rows - 1) + 2 * (chips - 1)
+        return [
+            pltpu.VMEM((rows, width), f32),
+            pltpu.VMEM((rows, width), f32),
+            pltpu.VMEM((half, width), f32),
+            pltpu.VMEM((grid_rows - 1, chunk, width), f32),
+            pltpu.VMEM((chips - 1, chunk // chips, width), f32),
+            DMA((copies,)),
+            DMA((copies,)),
+        ]
+
+    def start(self, source, target, device):
+        i = self.used
+        self.used += 1
+        copy = remote(source, target, self.send.at[i], self.recv.at[i], device)
+        copy.start()
+        self.pending.append(copy)
+        self.arrived.append(copy)
+
+    def landed(self):
+        arrived, self.arrived = self.arrived, []
+        for copy in arrived:
+            copy.wait_recv()
+
+    def rows_of(self, r):
+        return pl.ds(pl.multiple_of((self.g.k * self.g.rows + r) * self.chunk, self.chunk), self.chunk)
+
+    def unit_of(self, r, z):
+        at = ((self.g.k * self.g.rows + r) * self.g.chips + z) * self.unit
+        return pl.ds(pl.multiple_of(at, self.unit), self.unit)
+
+    def pair_out(self):
+        g = self.g
+        other = pl.ds(pl.multiple_of((1 - g.k) * self.half, self.half), self.half)
+        self.start(self.part.at[other], self.half_in, g.partner)
+
+    def stage_base(self, s):
+        return self.g.rows - 2 ** (self.g.stages - s)
+
+    def halve(self, s):
+        g = self.g
+        self.landed()
+        if s == 0:
+            mine = pl.ds(pl.multiple_of(g.k * self.half, self.half), self.half)
+            self.part[mine] += self.half_in[...]
+        else:
+            self.take(s - 1)
+        for j in range(g.count(s)):
+            rows = self.rows_of(g.block(s, j, g.peer_row(s)))
+            self.start(self.part.at[rows], self.stage_in.at[self.stage_base(s) + j], g.peer(s))
+
+    def take(self, s):
+        g = self.g
+        for j in range(g.count(s)):
+            self.part[self.rows_of(g.block(s, j, g.r))] += self.stage_in[self.stage_base(s) + j]
+
+    def chips_out(self):
+        g = self.g
+        self.landed()
+        self.take(g.stages - 1)
+        for w in range(g.chips - 1):
+            z = g.chip(w)[0]
+            self.start(self.part.at[self.unit_of(g.r, z)], self.chip_in.at[w], g.chip_device(z))
+
+    def chips_back(self):
+        g = self.g
+        self.landed()
+        own = self.unit_of(g.r, g.z)
+        total = self.part[own]
+        for w in range(g.chips - 1):
+            total = total + self.chip_in[w]
+        self.full[own] = total
+        for w in range(g.chips - 1):
+            self.start(self.full.at[own], self.full.at[own], g.chip_device(g.chip(w)[0]))
+
+    def double(self, s):
+        g = self.g
+        self.landed()
+        for j in range(g.count(s)):
+            rows = self.rows_of(g.block(s, j, g.r))
+            self.start(self.full.at[rows], self.full.at[rows], g.peer(s))
+
+    def pair_back(self):
+        g = self.g
+        self.landed()
+        mine = pl.ds(pl.multiple_of(g.k * self.half, self.half), self.half)
+        self.start(self.full.at[mine], self.full.at[mine], g.partner)
+
+    def finish(self):
+        self.landed()
+
+    def drain(self):
+        for copy in self.pending:
+            copy.wait_send()
+
+
+def reduce_kernel(rows, cols, part_ref, out_ref, *scratch):
+    grid = Grid(rows, cols)
+    grid.greet()
+    part, full, *rest = scratch
+    part[...] = part_ref[...]
+    total = AllReduce(grid, part, full, *rest)
+    for phase in total.phases:
+        phase()
+    out_ref[...] = full[...]
+    total.drain()
+
+
+def all_reduce(value, rows, cols, collective_id):
+    return pl.pallas_call(
+        functools.partial(reduce_kernel, rows, cols),
+        out_shape=jax.ShapeDtypeStruct(value.shape, f32),
+        in_specs=[VMEM],
+        out_specs=VMEM,
+        scratch_shapes=AllReduce.scratch(*value.shape, rows, cols // 2),
+        compiler_params=pltpu.CompilerParams(
+            collective_id=collective_id, has_side_effects=True, vmem_limit_bytes=vmem_bytes
+        ),
+        name="all_reduce",
+    )(value)
+
+
+def power_kernel(
+    rows, cols, acc, pair_ref, grads_ref, acts_ref, out_ref,
+    tiles, mine, theirs, pair_in, stage_in, chip_in,
+    tile_sem, pair_sems, stage_sems, chip_sems, *reduce_scratch,
+):
+    g = Grid(rows, cols)
+    blk = acts_ref.shape[0]
+    rank = out_ref.shape[0]
+    chips, stages = g.chips, g.stages
+
+    def chip_of(w):
+        return g.chip(w)[0]
+
+    def fetch(w, rp, kind):
+        core = (1 - g.k) if kind == 0 else g.k
+        at = ((rp * chips + (g.z + 1 + w) % chips) * 2 + core) * blk
+        columns = pl.ds(pl.multiple_of(at, blk), blk)
+        slot = (w * rows + rp) % 2
+        return pltpu.make_async_copy(
+            acc.at[:, columns], tiles.at[kind * 2 + slot], tile_sem.at[kind * 2 + slot]
+        )
+
+    for rp in range(2):
+        fetch(0, rp, 0).start()
+        fetch(0, rp, 1).start()
+    g.greet()
+
+    part, full, *rest = reduce_scratch
+    part[...] = mul(pair_ref[:rank], grads_ref[...], rows_cols) + mul(
+        pair_ref[rank:], grads_ref[...], rows_cols
+    )
+    tokens = AllReduce(g, part, full, *rest)
+    phases = iter(tokens.phases)
+
+    def tick():
+        phase = next(phases, None)
+        if phase is not None:
+            phase()
+
+    tick()
+
+    def product(slot):
+        upper, lower = split(tiles[slot])
+        both = mul(pair_ref[...], upper, rows_cols)
+        return both[:rank] + both[rank:] + mul(pair_ref[:rank], lower, rows_cols)
+
+    def pair_copy(w, rp):
+        i = w * rows + rp
+        return remote(theirs.at[i], pair_in.at[i], pair_sems.at[0, i], pair_sems.at[1, i], g.partner)
+
+    def stage_copy(w, s, j):
+        i = w * (rows - 1) + rows - 2 ** (stages - s) + j
+        source = mine.at[w * rows + g.block(s, j, g.peer_row(s))]
+        return remote(source, stage_in.at[i], stage_sems.at[0, i], stage_sems.at[1, i], g.peer(s))
+
+    def chip_copy(w):
+        return remote(
+            mine.at[w * rows + g.r], chip_in.at[w], chip_sems.at[0, w], chip_sems.at[1, w],
+            g.chip_device(chip_of(w)),
+        )
+
+    def compute(w):
+        def step(rp, carry):
+            i = w * rows + rp
+            slot = i % 2
+            for kind, store in ((0, theirs), (1, mine)):
+                fetch(w, rp, kind).wait()
+                store[i] = product(kind * 2 + slot)
+                if kind == 0:
+                    pair_copy(w, rp).start()
+
+                @pl.when(i + 2 < chips * rows)
+                def _():
+                    fetch((i + 2) // rows, (i + 2) % rows, kind).start()
+            return carry
+
+        lax.fori_loop(0, rows, step, 0)
+
+    def add(index, value_ref, at):
+        mine[index] += value_ref[at]
+
+    def halve(w, s):
+        if s == 0:
+            for base, send in ((g.peer_row(0), True), (g.r, False)):
+                for j in range(g.count(0)):
+                    rp = g.block(0, j, base)
+                    pair_copy(w, rp).wait_recv()
+                    add(w * rows + rp, pair_in, w * rows + rp)
+                    if send:
+                        stage_copy(w, 0, j).start()
+            return
+        for j in range(g.count(s - 1)):
+            i = w * (rows - 1) + rows - 2 ** (stages - s + 1) + j
+            stage_copy(w, s - 1, j).wait_recv()
+            add(w * rows + g.block(s - 1, j, g.r), stage_in, i)
+        for j in range(g.count(s)):
+            stage_copy(w, s, j).start()
+
+    def leave(w):
+        i = w * (rows - 1) + rows - 2
+        stage_copy(w, stages - 1, 0).wait_recv()
+        add(w * rows + g.r, stage_in, i)
+        if w < chips - 1:
+            chip_copy(w).start()
+
+    for at in range(chips + stages + 1):
+        if at < chips:
+            compute(at)
+        for later in range(1, stages + 1):
+            w = at - later
+            if 0 <= w < chips:
+                tick()
+                halve(w, later - 1)
+        w = at - stages - 1
+        if 0 <= w < chips:
+            tick()
+            leave(w)
+    for phase in phases:
+        phase()
+    upper, lower = split(full[...])
+    total = mul(upper, acts_ref[...], cols_cols) + mul(lower, acts_ref[...], cols_cols)
+    total = total + mine[(chips - 1) * rows + g.r]
+    for w in range(chips - 1):
+        chip_copy(w).wait_recv()
+        total = total + chip_in[w]
+    out_ref[...] = total
+
+    tokens.drain()
+    for w in range(chips):
+        def done(rp, carry):
+            pair_copy(w, rp).wait_send()
+            return carry
+
+        lax.fori_loop(0, rows, done, 0)
+        for s in range(stages):
+            for j in range(g.count(s)):
+                stage_copy(w, s, j).wait_send()
+        if w < chips - 1:
+            chip_copy(w).wait_send()
+
+
+def power_scatter(accumulated, pair, grads, acts, rows, cols, collective_id):
+    rank = pair.shape[0] // 2
+    blk = acts.shape[0]
+    chips = cols // 2
+    blocks = chips * rows
+    passed = chips * (rows - 1)
+    return pl.pallas_call(
+        functools.partial(power_kernel, rows, cols),
+        out_shape=jax.ShapeDtypeStruct((rank, blk), f32),
+        in_specs=[ANY, VMEM, VMEM, VMEM],
+        out_specs=VMEM,
+        scratch_shapes=[
+            pltpu.VMEM((4, accumulated.shape[0], blk), f32),
+            pltpu.VMEM((blocks, rank, blk), f32),
+            pltpu.VMEM((blocks, rank, blk), f32),
+            pltpu.VMEM((blocks, rank, blk), f32),
+            pltpu.VMEM((passed, rank, blk), f32),
+            pltpu.VMEM((chips - 1, rank, blk), f32),
+            DMA((4,)),
+            DMA((2, blocks)),
+            DMA((2, passed)),
+            DMA((2, chips - 1)),
+            *AllReduce.scratch(rank, acts.shape[1], rows, chips),
+        ],
+        compiler_params=pltpu.CompilerParams(
+            collective_id=collective_id, has_side_effects=True, vmem_limit_bytes=vmem_bytes
+        ),
+        name="power_scatter",
+    )(accumulated, pair, grads, acts)
 
 
 def solve_lower(gram_matrix, right):
@@ -52,7 +439,17 @@
     return jnp.concatenate(solved, axis=0)
 
 
-def body(activations, out_grads, accumulated, seed_basis, moment_first, moment_second):
+def finish(moment_first, moment_second, projected, full_basis):
+    first_next = beta_first * moment_first + (1.0 - beta_first) * projected
+    second_next = beta_second * moment_second + (1.0 - beta_second) * projected * projected
+    direction = (
+        first_next / correct_first / (jnp.sqrt(second_next / correct_second) + epsilon_value)
+    )
+    lifted = lift_scale * mul(direction.astype(bf16), full_basis, cols_cols)
+    return first_next, second_next, lifted
+
+
+def plain_body(activations, out_grads, accumulated, seed_basis, moment_first, moment_second):
     share_rows = activations.shape[0]
     acts = activations.astype(jnp.float32)
     grads = out_grads.astype(jnp.float32)
@@ -80,28 +477,51 @@
     projected = mul(accumulated.astype(jnp.bfloat16), full_basis, rows_cols) + mul(
         grads, basis_tokens, rows_cols, high
     )
-    first_next = beta_first * moment_first + (1.0 - beta_first) * projected
-    second_next = beta_second * moment_second + (1.0 - beta_second) * projected * projected
-    direction = (
-        first_next / correct_first / (jnp.sqrt(second_next / correct_second) + epsilon_value)
-    )
-    lifted = lift_scale * mul(direction.astype(jnp.bfloat16), full_basis, cols_cols)
-    return (basis_rows, first_next, second_next, lifted)
+    return (basis_rows, *finish(moment_first, moment_second, projected, full_basis))
+
+
+def body(rows, cols, activations, out_grads, accumulated, seed_basis, moment_first, moment_second):
+    share_rows = activations.shape[0]
+    reduce = functools.partial(all_reduce, rows=rows, cols=cols)
+    grads = out_grads.astype(jnp.float32)
+    own_seed = lax.dynamic_slice_in_dim(
+        seed_basis, lax.axis_index("col") * share_rows, share_rows, 0
+    )
+    acts = activations.astype(jnp.float32)
+    full_seed = lax.all_gather(own_seed, every, axis=0, tiled=True)
+    seed_tokens = reduce(mul(own_seed, acts, rows_rows, highest), collective_id=1)
+    image_turned = mul(full_seed, accumulated, ((0,), (1,)), high) + mul(
+        seed_tokens, grads, cols_cols, high
+    )
+    upper = lax.reduce_precision(image_turned, 8, 7)
+    pair = jnp.concatenate([upper, image_turned - upper], axis=0).astype(bf16)
+    power_turned = power_scatter(accumulated, pair, out_grads, activations, rows, cols, 2)
+    gram_matrix = reduce(mul(power_turned, power_turned, cols_cols, highest), collective_id=3)
+    solved = solve_lower(gram_matrix, power_turned)
+    basis_rows = solved.T.astype(jnp.bfloat16)
+    full_basis = lax.all_gather(basis_rows, every, axis=0, tiled=True)
+    basis_tokens = reduce(
+        mul(basis_rows, activations, rows_rows), collective_id=4
+    )
+    projected = mul(accumulated.astype(jnp.bfloat16), full_basis, rows_cols) + mul(
+        grads, basis_tokens, cols_cols, high
+    )
+    return (basis_rows, *finish(moment_first, moment_second, projected, full_basis))
 
 
 def solution(mesh):
-    in_specs = (
-        P(("row", "col"), None),
-        P(("row", "col"), None),
-        P(("row", "col"), None),
-        P("row", None),
-        P(("row", "col"), None),
-        P(("row", "col"), None),
-    )
-    out_specs = (
-        P(("row", "col"), None),
-        P(("row", "col"), None),
-        P(("row", "col"), None),
-        P(("row", "col"), None),
-    )
-    return jax.shard_map(body, mesh=mesh, in_specs=in_specs, out_specs=out_specs, check_vma=False)
+    rows, cols = mesh.shape["row"], mesh.shape["col"]
+
+    def place(activations, *others):
+        rank = others[2].shape[1]
+        fits = rows & (rows - 1) == 0 and rows > 1 and cols % 2 == 0 and cols > 2
+        fits = fits and activations.shape[0] % 128 == 0 and rank % (8 * rows * cols) == 0
+        if fits:
+            return body(rows, cols, activations, *others)
+        return plain_body(activations, *others)
+
+    split_rows = P(("row", "col"), None)
+    in_specs = (split_rows, split_rows, split_rows, P("row", None), split_rows, split_rows)
+    return jax.shard_map(
+        place, mesh=mesh, in_specs=in_specs, out_specs=(split_rows,) * 4, check_vma=False
+    )

time: 1070 us -> 633 us (0.59)
  waiting for transfers between devices: 756 us -> 65.7 us
  Pallas kernels: 0 us -> 308 us
  matrix products: 182 us -> 130 us
    psum x3 -> x0, waiting for transfers between devices: 362 us -> none  [the longest x1 134 us: body(): seed_tokens = lax.psum(mul(acts, own_seed, rows_rows, highest), every)]
    pallas_call x0 -> x4, Pallas kernels: none -> 308 us  [the longest x3 169 us: all_reduce(): pl.pallas_call(functools.partial(reduce_kernel, rows, cols), out_shape=ja...]
    reduce_scatter x1 -> x0, waiting for transfers between devices: 188 us -> none  [body(): lax.psum_scatter(power_part, every, scatter_dimension=0, tiled=True)]
    all_gather x2 -> x1, waiting for transfers between devices: 92.9 us -> 15.6 us  [body(): full_basis = lax.all_gather(basis_rows, every, axis=0, tiled=True)]
    all_gather x1, waiting for transfers between devices: 113 us -> 50 us  [body(): full_seed = lax.all_gather(own_seed, every, axis=0, tiled=True)]
    dot_general x37 -> x34, matrix products: 181 us -> 128 us  [mul(): lax.dot_general(left, right, (dims, ((), ())), precision=precision, prefe...]
  transfers between devices with their start and end apart: 7 -> 2, of which waited for: 7 -> 2; matrix products, arithmetic and copies ran while one was open for 14% -> 2% of each run, Pallas kernels for 0% -> 21%
where the time goes in v1:
time: 633 us; the launch traced here: 625 us
  Pallas kernels  308 us (49%)
  matrix products  130 us (21%)
  other arithmetic  93.7 us (15%)
  waiting for transfers between devices  65.7 us (10%)
  between operations  14.8 us (2%)
  local copies, waits for them, and re-layouts  12.5 us (2%)
    pallas_call x3, Pallas kernels, all_reduce(): pl.pallas_call(functools.partial(reduce_kernel, rows, cols), out_shape=ja...  169 us
    pallas_call x1, Pallas kernels, power_scatter(): pl.pallas_call(functools.partial(power_kernel, rows, cols), out_shape=jax...  139 us
    dot_general x34, matrix products, mul(): lax.dot_general(left, right, (dims, ((), ())), precision=precision, prefe...  128 us
    all_gather x1, waiting for transfers between devices, body(): full_seed = lax.all_gather(own_seed, every, axis=0, tiled=True)  50 us
    another operation x12, other arithmetic, solve_lower(): factor = lax.linalg.cholesky(trailing[j, j], symmetrize_input=False)  49.7 us
    another operation x8, other arithmetic, solve_lower(): jax.scipy.linalg.solve_triangular(factor, jnp.eye(step, dtype=jnp.float32...  41.9 us
    all_gather x1, waiting for transfers between devices, body(): full_basis = lax.all_gather(basis_rows, every, axis=0, tiled=True)  15.6 us
  transfers between devices with their start and end apart: 2, of which 2 were waited for; matrix products, arithmetic and copies ran while one was open for 2% of the time, Pallas kernels for 21%

profile of v1, /device:TPU:25, one launch (start us, length us, event | category | flops | bytes accessed | tf_op | source)
XLA Modules:
  0.0 624.6 jit_solution(10859733754231577670)
XLA Ops:
  7.2 1.9 constant_dynamic-slice_fusion
  9.2 3.4 fusion.41.part_ref
  12.6 63.3 %all_reduce.3 = f32[512,1024]{1,0:T(8,128)} custom-call(f32[512,1024]{1,0:T(8,128)} %fusion.41.part_ref), custom_call_target="tpu_custom_call" | custom-call | tf_op jit(solution)/shard_map/all_reduce/pallas_call | solution.py:231
  76.0 4.5 fusion.42
  80.5 50.0 %all-gather.3.cloned.1.call-done = f32[8192,512]{1,0:T(8,128)} async-done(((f32[256,512]{1,0:T(8,128)}), f32[8192,512]{1,0:T(8,128)}) %all-gather.3.cloned.1.call-update) | async-done | bytes 16777232 | tf_op jit(solution)/shard_map/all_gather | solution.py:491
  130.5 57.6 %reduce-precision_convert_fusion = (bf16[512,896]{1,0:T(8,128)(2,1)S(1)}, bf16[512,896]{1,0:T(8,128)(2,1)S(1)}) fusion(f32[512,896]{1,0:T(8,128)S(1)} %fusion.42, f32[8192,512]{1,0:T(8,128)} %all-gather.3.cloned.1.call-done, f32[896,8192]{1,0:T(8,128)} %acc.1), kind=kOutput, calls=%fused_computation.5 | convolution fusion | flops 22550872064 | bytes 49807360 | tf_op jit(solution)/shard_map/dot_general | solution.py:30
  189.5 139.4 %power_scatter.1 = f32[512,256]{1,0:T(8,128)} custom-call(f32[896,8192]{1,0:T(8,128)} %acc.1, bf16[1024,896]{1,0:T(8,128)(2,1)} %pad_maximum_fusion.pair_ref, bf16[896,1024]{1,0:T(8,128)(2,1)} %grads_ref.1, bf16[256,1024]{1,0:T(8,128)(2,1)} %acts_ref.1), custom_call_target="tpu_custom_call" | custom-call | tf_op jit(solution)/shard_map/power_scatter/pallas_call | solution.py:391
  329.0 3.3 fusion.43.part_ref
  332.2 36.6 %all_reduce.4 = f32[512,512]{1,0:T(8,128)} custom-call(f32[512,512]{1,0:T(8,128)} %fusion.43.part_ref), custom_call_target="tpu_custom_call" | custom-call | tf_op jit(solution)/shard_map/all_reduce/pallas_call | solution.py:231
  369.6 11.7 %custom-call.12 = f32[128,128]{1,0:T(8,128)S(1)} custom-call(f32[128,128]{1,0:T(8,128)S(1)} %slice.48), custom_call_target="Cholesky" | custom-call | tf_op jit(solution)/shard_map/cholesky/custom-call.1 | solution.py:427
  382.7 9.8 %custom-call.13 = f32[1,128,128]{1,2,0:T(8,128)S(1)} custom-call(f32[1,128,128]{2,1,0:T(8,128)S(1)} %fusion.18), custom_call_target="InvertDiagBlocksLowerTriangular" | custom-call | tf_op jit(solution)/shard_map/jit(_solve_triangular)/triangular_solve | solution.py:428
  403.8 11.9 %custom-call.14 = f32[128,128]{1,0:T(8,128)S(1)} custom-call(f32[128,128]{1,0:T(8,128)S(1)} %convolution_subtract_fusion.15), custom_call_target="Cholesky" | custom-call | tf_op jit(solution)/shard_map/cholesky/custom-call.1 | solution.py:427
  417.1 9.8 %custom-call.15 = f32[1,128,128]{1,2,0:T(8,128)S(1)} custom-call(f32[1,128,128]{2,1,0:T(8,128)S(1)} %fusion.19), custom_call_target="InvertDiagBlocksLowerTriangular" | custom-call | tf_op jit(solution)/shard_map/jit(_solve_triangular)/triangular_solve | solution.py:428
  428.0 11.7 %custom-call.16 = f32[128,128]{1,0:T(8,128)S(1)} custom-call(f32[128,128]{1,0:T(8,128)S(1)} %convolution_subtract_fusion.12), custom_call_target="Cholesky" | custom-call | tf_op jit(solution)/shard_map/cholesky/custom-call.1 | solution.py:427
  441.0 9.8 %custom-call.17 = f32[1,128,128]{1,2,0:T(8,128)S(1)} custom-call(f32[1,128,128]{2,1,0:T(8,128)S(1)} %fusion.20), custom_call_target="InvertDiagBlocksLowerTriangular" | custom-call | tf_op jit(solution)/shard_map/jit(_solve_triangular)/triangular_solve | solution.py:428
  453.5 11.7 %custom-call.18 = f32[128,128]{1,0:T(8,128)S(1)} custom-call(f32[128,128]{1,0:T(8,128)S(1)} %convolution_subtract_fusion.6), custom_call_target="Cholesky" | custom-call | tf_op jit(solution)/shard_map/cholesky/custom-call.1 | solution.py:427
  466.6 9.8 %custom-call.19 = f32[1,128,128]{1,2,0:T(8,128)S(1)} custom-call(f32[1,128,128]{2,1,0:T(8,128)S(1)} %fusion.21), custom_call_target="InvertDiagBlocksLowerTriangular" | custom-call | tf_op jit(solution)/shard_map/jit(_solve_triangular)/triangular_solve | solution.py:428
  479.7 2.8 copy.11
  485.1 69.0 %all_reduce.5 = f32[512,1024]{1,0:T(8,128)} custom-call(f32[512,1024]{1,0:T(8,128)} %fusion.32.part_ref), custom_call_target="tpu_custom_call" | custom-call | tf_op jit(solution)/shard_map/all_reduce/pallas_call | solution.py:231
  554.1 15.6 %all-gather.5.cloned.1.call-done = bf16[8192,512]{0,1:T(8,128)(2,1)} async-done(((bf16[256,512]{0,1:T(8,128)(2,1)}), bf16[8192,512]{0,1:T(8,128)(2,1)}) %all-gather.5.cloned.1.call-update) | async-done | bytes 8388624 | tf_op jit(solution)/shard_map/all_gather | solution.py:502
  569.7 17.8 %fusion = f32[512,896]{1,0:T(8,128)} fusion(bf16[8192,512]{0,1:T(8,128)(2,1)} %all-gather.5.cloned.1.call-done, f32[896,8192]{1,0:T(8,128)} %acc.1), kind=kOutput, calls=%fused_computation.1 | convolution fusion | flops 7523532800 | bytes 39583744 | tf_op jit(solution)/shard_map/dot_general | solution.py:30
  587.5 7.7 %fusion.3 = (f32[896,512]{0,1:T(8,128)S(1)}, f32[896,512]{0,1:T(8,128)}) fusion(f32[896,512]{0,1:T(8,128)} %copy.11, f32[896,512]{0,1:T(8,128)} %copy.10, f32[512,896]{1,0:T(8,128)} %fusion, f32[512,1024]{1,0:T(8,128)} %all_reduce.5, bf16[896,1024]{1,0:T(8,128)(2,1)} %grads_ref.1), kind=kOutput, calls=%fused_computation.7 | convolution fusion | flops 2822242304 | bytes 13107200 | tf_op jit(solution)/shard_map/dot_general | solution.py:30
  595.2 2.7 copy.13
  599.6 17.7 %convolution_multiply_fusion = f32[896,8192]{1,0:T(8,128)} fusion(bf16[8192,512]{0,1:T(8,128)(2,1)} %all-gather.5.cloned.1.call-done, f32[896,512]{0,1:T(8,128)S(1)} %get-tuple-element.10, f32[896,512]{0,1:T(8,128)} %get-tuple-element.11), kind=kOutput, calls=%fused_computation | convolution fusion | flops 7525826560 | bytes 41418752 | tf_op jit(solution)/shard_map/dot_general | solution.py:30
  (63 shorter events, 30.2 us)
Async XLA Ops:
  7.2 2.1 copy-start.1
  7.2 123.3 %all-gather.3.cloned.1.call-start = ((), (), s32[]{:S(2)}) async-start(), calls=%async_computation | async-start | bytes 17301504 | tf_op jit(solution)/shard_map/all_gather | solution.py:491
  9.2 560.6 %all-gather.5.cloned.1.call-start = ((), (), s32[]{:S(2)}) async-start(), calls=%async_computation.1 | async-start | bytes 8650752 | tf_op jit(solution)/shard_map/all_gather | solution.py:502
  328.9 63.8 %copy-start = (f32[512,256]{1,0:T(8,128)S(1)}, f32[512,256]{1,0:T(8,128)}, u32[]{:S(2)}) copy-start(f32[512,256]{1,0:T(8,128)} %power_scatter.1) | copy-start | bytes 1572868
  451.7 26.3 %copy-start.4 = (f32[896,512]{1,0:T(8,128)S(1)}, f32[896,512]{1,0:T(8,128)}, u32[]{:S(2)}) copy-start(f32[896,512]{1,0:T(8,128)} %param.13) | copy-start | bytes 5505028
  479.6 2.8 copy-start.3
  479.7 3.6 copy-start.2
Sparse Core Ops, SparseCore 0:
  11.6 118.8 all-gather.2
  478.1 91.6 all-gather.4

commit v2 on v1

--- a/solution.py
+++ b/solution.py
@@ -413,6 +413,337 @@
     )(accumulated, pair, grads, acts)
 
 
+class Interleaved:
+    def __init__(self, phases):
+        self.left = list(phases)
+
+    def tick(self, count=1):
+        for _ in range(count):
+            if self.left:
+                self.left.pop(0)()
+
+    def rest(self):
+        self.tick(len(self.left))
+
+
+def image_kernel(
+    rows, cols, acc, seed_ref, grads_ref, acts_ref, out_ref,
+    tiles, image, seeds, tile_sem, pair_sems, stage_sems, *reduce_scratch,
+):
+    g = Grid(rows, cols)
+    stages = g.stages
+    blk, rank = seeds.shape[2], seeds.shape[3]
+    own_rows = seed_ref.shape[0]
+    pieces = own_rows // (2 * blk)
+    tokens_rows = acts_ref.shape[0]
+
+    def piece(rp, h, i):
+        return (rp * 2 + h) * pieces + i
+
+    def fetch(p, slot):
+        columns = pl.ds(pl.multiple_of(p * blk, blk), blk)
+        return pltpu.make_async_copy(acc.at[:, columns], tiles.at[slot], tile_sem.at[slot])
+
+    def order(t):
+        u = t - 2 * pieces
+        wave = u // (2 * (rows - 1))
+        inner = u % (2 * (rows - 1))
+        other = piece((g.r + 1 + inner // 2) % rows, inner % 2, wave)
+        own = piece(g.r, t // pieces, t % pieces)
+        return jnp.where(t < 2 * pieces, own, other)
+
+    count = 2 * pieces * rows
+    depth = tiles.shape[0]
+    for t in range(depth - 1):
+        fetch(order(t), t).start()
+    g.greet()
+
+    own = pl.ds(pl.multiple_of(g.c * tokens_rows, tokens_rows), tokens_rows)
+    turned = seed_ref[own].T
+    part, full, *rest = reduce_scratch
+    upper, lower = split(turned)
+    part[...] = mul(upper, acts_ref[...], rows_cols) + mul(lower, acts_ref[...], rows_cols)
+    tokens = AllReduce(g, part, full, *rest)
+    small = Interleaved(tokens.phases)
+    small.tick()
+
+    def spread(q, carry):
+        at = pl.ds(pl.multiple_of(q * blk, blk), blk)
+        upper, lower = split(seed_ref[at])
+        target = g.r * 2 * pieces + q
+        seeds[target, 0] = upper
+        seeds[target, 1] = lower
+        return carry
+
+    lax.fori_loop(0, 2 * pieces, spread, 0)
+
+    def pair_copy(rp, i):
+        p = piece(rp, g.k, i)
+        at = i * rows + rp
+        return remote(seeds.at[p], seeds.at[p], pair_sems.at[0, at], pair_sems.at[1, at], g.partner)
+
+    def pair_wait(rp, i):
+        at = i * rows + rp
+        p = piece(rp, 1 - g.k, i)
+        remote(seeds.at[p], seeds.at[p], pair_sems.at[0, at], pair_sems.at[1, at], g.partner).wait_recv()
+
+    def stage_copy(i, s, j, base):
+        at = i * (rows - 1) + rows - 2 ** (stages - s) + j
+        p = piece(g.block(s, j, base), g.k, i)
+        return remote(seeds.at[p], seeds.at[p], stage_sems.at[0, at], stage_sems.at[1, at], g.peer(s))
+
+    def send(i, s):
+        for j in range(g.count(s)):
+            stage_copy(i, s, j, g.r).start()
+
+    def land(i, s):
+        for j in range(g.count(s)):
+            stage_copy(i, s, j, g.peer_row(s)).wait_recv()
+            pair_copy(g.block(s, j, g.peer_row(s)), i).start()
+
+    def compute(t):
+        slot = t % depth
+        p = order(t)
+        fetch(p, slot).wait()
+
+        @pl.when(t + depth - 1 < count)
+        def _():
+            fetch(order(t + depth - 1), (t + depth - 1) % depth).start()
+
+        upper, lower = split(tiles[slot])
+        image[...] += (
+            mul(upper, seeds[p, 0], rows_cols)
+            + mul(lower, seeds[p, 0], rows_cols)
+            + mul(upper, seeds[p, 1], rows_cols)
+        )
+
+    def own_step(t, carry):
+        compute(t)
+        return carry
+
+    def other_step(t, carry):
+        inner = (t - 2 * pieces) % (2 * (rows - 1))
+        wave = (t - 2 * pieces) // (2 * (rows - 1))
+        rp = (g.r + 1 + inner // 2) % rows
+
+        @pl.when(inner % 2 == 1 - g.k)
+        def _():
+            pair_wait(rp, wave)
+
+        compute(t)
+        return carry
+
+    image[...] = jnp.zeros_like(image)
+    for i in range(pieces):
+        send(i, stages - 1)
+    first = 2 * pieces // (stages + 1)
+    done = 0
+    lag = stages
+    for at in range(pieces + lag):
+        small.tick(2)
+        for late in range(stages):
+            i = at - late
+            if 0 <= i < pieces:
+                s = stages - 1 - late
+                land(i, s)
+                if s > 0:
+                    send(i, s - 1)
+        if done < 2 * pieces:
+            stop = min(2 * pieces, done + first)
+            lax.fori_loop(done, stop, own_step, 0)
+            done = stop
+        i = at - lag
+        if 0 <= i < pieces:
+            lax.fori_loop(done, 2 * pieces, own_step, 0)
+            done = 2 * pieces
+            start = 2 * pieces + i * 2 * (rows - 1)
+            lax.fori_loop(start, start + 2 * (rows - 1), other_step, 0)
+    small.rest()
+    upper, lower = split(full[...])
+    total = image[...] + mul(grads_ref[...], upper, cols_cols) + mul(grads_ref[...], lower, cols_cols)
+    upper, lower = split(total.T)
+    out_ref[:rank] = upper
+    out_ref[rank:] = lower
+
+    tokens.drain()
+    for i in range(pieces):
+        for s in range(stages):
+            for j in range(g.count(s)):
+                stage_copy(i, s, j, g.r).wait_send()
+                pair_copy(g.block(s, j, g.peer_row(s)), i).wait_send()
+
+
+def image_pair(accumulated, seed, grads, acts, rows, cols, collective_id):
+    rank = seed.shape[1]
+    height, width = accumulated.shape
+    blk = 256 if seed.shape[0] % 512 == 0 else seed.shape[0] // 2
+    total = width // blk
+    pieces = total // (2 * rows)
+    return pl.pallas_call(
+        functools.partial(image_kernel, rows, cols),
+        out_shape=jax.ShapeDtypeStruct((2 * rank, height), bf16),
+        in_specs=[ANY, VMEM, VMEM, VMEM],
+        out_specs=VMEM,
+        scratch_shapes=[
+            pltpu.VMEM((4, height, blk), f32),
+            pltpu.VMEM((height, rank), f32),
+            pltpu.VMEM((total, 2, blk, rank), bf16),
+            DMA((4,)),
+            DMA((2, pieces * rows)),
+            DMA((2, pieces * (rows - 1))),
+            *AllReduce.scratch(rank, acts.shape[1], rows, cols // 2),
+        ],
+        compiler_params=pltpu.CompilerParams(
+            collective_id=collective_id, has_side_effects=True, vmem_limit_bytes=vmem_bytes
+        ),
+        name="image_pair",
+    )(accumulated, seed, grads, acts)
+
+
+def project_kernel(
+    rows, cols, acc, basis_ref, turned_ref, grads_ref, acts_ref, out_ref, full_ref,
+    tiles, tile_sem, pair_sems, stage_sems, chip_sems, *reduce_scratch,
+):
+    g = Grid(rows, cols)
+    chips, stages = g.chips, g.stages
+    blk = basis_ref.shape[0]
+    count = chips * rows
+
+    def chip_of(w):
+        return (g.z + chips - w) % chips
+
+    def at_of(rp, w, core):
+        at = ((rp * chips + chip_of(w)) * 2 + core) * blk
+        return full_ref.at[pl.ds(pl.multiple_of(at, blk), blk)]
+
+    def fetch(t):
+        w, rp = t // rows, t % rows
+        at = (rp * chips + chip_of(w)) * 2 * blk
+        columns = pl.ds(pl.multiple_of(at, 2 * blk), 2 * blk)
+        return pltpu.make_async_copy(acc.at[:, columns], tiles.at[t % 2], tile_sem.at[t % 2])
+
+    fetch(0).start()
+    fetch(1).start()
+    g.greet()
+    own_rows = pl.ds(pl.multiple_of(((g.r * chips + g.z) * 2 + g.k) * blk, blk), blk)
+    full_ref[own_rows] = basis_ref[...]
+
+    def pair_copy(rp, w):
+        i = w * rows + rp
+        ref = at_of(rp, w, g.k)
+        return remote(ref, ref, pair_sems.at[0, i], pair_sems.at[1, i], g.partner)
+
+    def pair_wait(rp, w):
+        i = w * rows + rp
+        ref = at_of(rp, w, 1 - g.k)
+        remote(ref, ref, pair_sems.at[0, i], pair_sems.at[1, i], g.partner).wait_recv()
+
+    def stage_copy(w, s, j, base):
+        i = w * (rows - 1) + rows - 2 ** (stages - s) + j
+        ref = at_of(g.block(s, j, base), w, g.k)
+        return remote(ref, ref, stage_sems.at[0, i], stage_sems.at[1, i], g.peer(s))
+
+    def chip_copy(w, z):
+        at = ((g.r * chips + z) * 2 + g.k) * blk
+        ref = full_ref.at[pl.ds(pl.multiple_of(at, blk), blk)]
+        return remote(
+            ref, ref, chip_sems.at[0, w], chip_sems.at[1, w], g.chip_device(g.chip(w)[0])
+        )
+
+    def enter(w):
+        if w > 0:
+            chip_copy(w - 1, chip_of(w)).wait_recv()
+        stage_copy(w, stages - 1, 0, g.r).start()
+        pair_copy(g.r, w).start()
+
+    def land(w, s):
+        for j in range(g.count(s)):
+            stage_copy(w, s, j, g.peer_row(s)).wait_recv()
+        if s > 0:
+            for j in range(g.count(s - 1)):
+                stage_copy(w, s - 1, j, g.r).start()
+        for j in range(g.count(s)):
+            pair_copy(g.block(s, j, g.peer_row(s)), w).start()
+
+    for w in range(chips - 1):
+        chip_copy(w, g.z).start()
+    part, full, *rest = reduce_scratch
+    enter(0)
+    part[...] = mul(turned_ref[...], acts_ref[...], rows_cols)
+    tokens = AllReduce(g, part, full, *rest)
+    small = Interleaved(tokens.phases)
+    small.tick()
+    out_ref[...] = jnp.zeros_like(out_ref)
+
+    def step(t, carry):
+        w, rp = t // rows, t % rows
+        fetch(t).wait()
+        pair_wait(rp, w)
+        at = (rp * chips + chip_of(w)) * 2 * blk
+        block = full_ref[pl.ds(pl.multiple_of(at, 2 * blk), 2 * blk)]
+        out_ref[...] += mul(tiles[t % 2].astype(bf16), block, rows_cols)
+
+        @pl.when(t + 2 < count)
+        def _():
+            fetch(t + 2).start()
+
+        return carry
+
+    for at in range(chips + stages + 1):
+        small.tick()
+        for late in range(stages + 1):
+            w = at - late
+            if 0 <= w < chips:
+                if late == 0:
+                    if w > 0:
+                        enter(w)
+                else:
+                    land(w, stages - late)
+        w = at - stages
+        if 0 <= w < chips:
+            lax.fori_loop(w * rows, (w + 1) * rows, step, 0)
+    small.rest()
+    upper, lower = split(full[...])
+    out_ref[...] += mul(grads_ref[...], upper, cols_cols) + mul(grads_ref[...], lower, cols_cols)
+
+    tokens.drain()
+    for w in range(chips - 1):
+        chip_copy(w, g.z).wait_send()
+    for w in range(chips):
+        pair_copy(g.r, w).wait_send()
+        for s in range(stages):
+            for j in range(g.count(s)):
+                stage_copy(w, s, j, g.r).wait_send()
+                pair_copy(g.block(s, j, g.peer_row(s)), w).wait_send()
+
+
+def project(accumulated, basis, turned, grads, acts, rows, cols, collective_id):
+    height, width = accumulated.shape
+    blk, rank = basis.shape
+    chips = cols // 2
+    return pl.pallas_call(
+        functools.partial(project_kernel, rows, cols),
+        out_shape=(
+            jax.ShapeDtypeStruct((height, rank), f32),
+            jax.ShapeDtypeStruct((width, rank), bf16),
+        ),
+        in_specs=[ANY, VMEM, VMEM, VMEM, VMEM],
+        out_specs=(VMEM, VMEM),
+        scratch_shapes=[
+            pltpu.VMEM((2, height, 2 * blk), f32),
+            DMA((2,)),
+            DMA((2, chips * rows)),
+            DMA((2, chips * (rows - 1))),
+            DMA((2, chips - 1)),
+            *AllReduce.scratch(rank, acts.shape[1], rows, chips),
+        ],
+        compiler_params=pltpu.CompilerParams(
+            collective_id=collective_id, has_side_effects=True, vmem_limit_bytes=vmem_bytes
+        ),
+        name="project",
+    )(accumulated, basis, turned, grads, acts)
+
+
 def solve_lower(gram_matrix, right):
     rank = gram_matrix.shape[0]
     step = 128 if rank % 128 == 0 else rank
@@ -481,31 +812,15 @@
 
 
 def body(rows, cols, activations, out_grads, accumulated, seed_basis, moment_first, moment_second):
-    share_rows = activations.shape[0]
-    reduce = functools.partial(all_reduce, rows=rows, cols=cols)
-    grads = out_grads.astype(jnp.float32)
-    own_seed = lax.dynamic_slice_in_dim(
-        seed_basis, lax.axis_index("col") * share_rows, share_rows, 0
+    common = (out_grads, activations, rows, cols)
+    pair = image_pair(accumulated, seed_basis, *common, 1)
+    power_turned = power_scatter(accumulated, pair, *common, 2)
+    gram_matrix = all_reduce(
+        mul(power_turned, power_turned, cols_cols, highest), rows, cols, 3
     )
-    acts = activations.astype(jnp.float32)
-    full_seed = lax.all_gather(own_seed, every, axis=0, tiled=True)
-    seed_tokens = reduce(mul(own_seed, acts, rows_rows, highest), collective_id=1)
-    image_turned = mul(full_seed, accumulated, ((0,), (1,)), high) + mul(
-        seed_tokens, grads, cols_cols, high
-    )
-    upper = lax.reduce_precision(image_turned, 8, 7)
-    pair = jnp.concatenate([upper, image_turned - upper], axis=0).astype(bf16)
-    power_turned = power_scatter(accumulated, pair, out_grads, activations, rows, cols, 2)
-    gram_matrix = reduce(mul(power_turned, power_turned, cols_cols, highest), collective_id=3)
-    solved = solve_lower(gram_matrix, power_turned)
-    basis_rows = solved.T.astype(jnp.bfloat16)
-    full_basis = lax.all_gather(basis_rows, every, axis=0, tiled=True)
-    basis_tokens = reduce(
-        mul(basis_rows, activations, rows_rows), collective_id=4
-    )
-    projected = mul(accumulated.astype(jnp.bfloat16), full_basis, rows_cols) + mul(
-        grads, basis_tokens, cols_cols, high
-    )
+    turned = solve_lower(gram_matrix, power_turned).astype(bf16)
+    basis_rows = turned.T
+    projected, full_basis = project(accumulated, basis_rows, turned, *common, 4)
     return (basis_rows, *finish(moment_first, moment_second, projected, full_basis))
 
 

time: 633 us -> 513 us (0.81)
  matrix products: 130 us -> 37.1 us
  waiting for transfers between devices: 65.7 us -> 0 us
  Pallas kernels: 308 us -> 366 us
  between operations: 14.8 us -> 1.3 us
  local copies, waits for them, and re-layouts: 12.5 us -> 1.7 us
    pallas_call x0 -> x2, Pallas kernels: none -> 190 us  [the longest x1 117 us: image_pair(): pl.pallas_call(functools.partial(image_kernel, rows, cols), out_shape=jax...]
    pallas_call x3 -> x1, Pallas kernels: 169 us -> 35.3 us  [all_reduce(): pl.pallas_call(functools.partial(reduce_kernel, rows, cols), out_shape=ja...]
    dot_general x34 -> x28, matrix products: 128 us -> 36 us  [mul(): lax.dot_general(left, right, (dims, ((), ())), precision=precision, prefe...]
    all_gather x2 -> x0, waiting for transfers between devices: 65.7 us -> none  [the longest x1 50 us: body(): full_seed = lax.all_gather(own_seed, every, axis=0, tiled=True)]
    unnamed x15 -> x5, local copies, waits for them, and re-layouts: 9.74 us -> 0.85 us
  transfers between devices with their start and end apart: 2 -> 0, of which waited for: 2 -> 0; matrix products, arithmetic and copies ran while one was open for 2% -> 0% of each run, Pallas kernels for 21% -> 0%
where the time goes in v2:
time: 513 us; the launch traced here: 503 us
  Pallas kernels  366 us (71%)
  other arithmetic  97 us (19%)
  matrix products  37.1 us (7%)
    pallas_call x1, Pallas kernels, power_scatter(): pl.pallas_call(functools.partial(power_kernel, rows, cols), out_shape=jax...  141 us
    pallas_call x1, Pallas kernels, image_pair(): pl.pallas_call(functools.partial(image_kernel, rows, cols), out_shape=jax...  117 us
    pallas_call x1, Pallas kernels, project(): pl.pallas_call(functools.partial(project_kernel, rows, cols), out_shape=(...  73.5 us
    another operation x12, other arithmetic, solve_lower(): factor = lax.linalg.cholesky(trailing[j, j], symmetrize_input=False)  49.9 us
    another operation x8, other arithmetic, solve_lower(): jax.scipy.linalg.solve_triangular(factor, jnp.eye(step, dtype=jnp.float32...  41.9 us
    dot_general x28, matrix products, mul(): lax.dot_general(left, right, (dims, ((), ())), precision=precision, prefe...  36 us
    pallas_call x1, Pallas kernels, all_reduce(): pl.pallas_call(functools.partial(reduce_kernel, rows, cols), out_shape=ja...  35.3 us

profile of v2, /device:TPU:25, one launch (start us, length us, event | category | flops | bytes accessed | tf_op | source)
XLA Modules:
  0.0 503.5 jit_solution(18045545249998412665)
XLA Ops:
  0.6 116.9 %image_pair.1.pair_ref = bf16[1024,896]{1,0:T(8,128)(2,1)} custom-call(f32[896,8192]{1,0:T(8,128)} %acc.5, f32[2048,512]{1,0:T(8,128)} %seed_ref.1, bf16[896,1024]{1,0:T(8,128)(2,1)} %grads_ref.5, bf16[256,1024]{1,0:T(8,128)(2,1)} %acts_ref.5), custom_call_target="tpu_custom_call" | custom-call | tf_op jit(solution)/shard_map/image_pair/pallas_call | solution.py:582
  117.5 140.6 %power_scatter.1 = f32[512,256]{1,0:T(8,128)} custom-call(f32[896,8192]{1,0:T(8,128)} %acc.5, bf16[1024,896]{1,0:T(8,128)(2,1)} %image_pair.1.pair_ref, bf16[896,1024]{1,0:T(8,128)(2,1)} %grads_ref.5, bf16[256,1024]{1,0:T(8,128)(2,1)} %acts_ref.5), custom_call_target="tpu_custom_call" | custom-call | tf_op jit(solution)/shard_map/power_scatter/pallas_call | solution.py:391
  258.2 3.2 fusion.35.part_ref
  261.4 35.3 %all_reduce.1 = f32[512,512]{1,0:T(8,128)} custom-call(f32[512,512]{1,0:T(8,128)} %fusion.35.part_ref), custom_call_target="tpu_custom_call" | custom-call | tf_op jit(solution)/shard_map/all_reduce/pallas_call | solution.py:231
  297.5 11.7 %custom-call.12 = f32[128,128]{1,0:T(8,128)S(1)} custom-call(f32[128,128]{1,0:T(8,128)S(1)} %slice.48), custom_call_target="Cholesky" | custom-call | tf_op jit(solution)/shard_map/cholesky/custom-call.1 | solution.py:758
  310.6 9.8 %custom-call.13 = f32[1,128,128]{1,2,0:T(8,128)S(1)} custom-call(f32[1,128,128]{2,1,0:T(8,128)S(1)} %fusion.14), custom_call_target="InvertDiagBlocksLowerTriangular" | custom-call | tf_op jit(solution)/shard_map/jit(_solve_triangular)/triangular_solve | solution.py:759
  320.7 1.1 fusion.22
  321.8 1.1 fusion.24
  322.9 1.1 fusion.26
  324.0 1.1 convolution_subtract_fusion.10
  325.1 1.1 convolution_subtract_fusion.13
  326.2 1.2 convolution_subtract_fusion.15
  327.4 11.9 %custom-call.14 = f32[128,128]{1,0:T(8,128)S(1)} custom-call(f32[128,128]{1,0:T(8,128)S(1)} %convolution_subtract_fusion.15), custom_call_target="Cholesky" | custom-call | tf_op jit(solution)/shard_map/cholesky/custom-call.1 | solution.py:758
  340.6 9.8 %custom-call.15 = f32[1,128,128]{1,2,0:T(8,128)S(1)} custom-call(f32[1,128,128]{2,1,0:T(8,128)S(1)} %fusion.15), custom_call_target="InvertDiagBlocksLowerTriangular" | custom-call | tf_op jit(solution)/shard_map/jit(_solve_triangular)/triangular_solve | solution.py:759
  351.2 1.1 convolution_subtract_fusion.8
  352.6 1.1 convolution_subtract_fusion.14
  353.7 1.1 convolution_subtract_fusion.11
  355.4 11.7 %custom-call.16 = f32[128,128]{1,0:T(8,128)S(1)} custom-call(f32[128,128]{1,0:T(8,128)S(1)} %convolution_subtract_fusion.12), custom_call_target="Cholesky" | custom-call | tf_op jit(solution)/shard_map/cholesky/custom-call.1 | solution.py:758
  368.4 9.8 %custom-call.17 = f32[1,128,128]{1,2,0:T(8,128)S(1)} custom-call(f32[1,128,128]{2,1,0:T(8,128)S(1)} %fusion.16), custom_call_target="InvertDiagBlocksLowerTriangular" | custom-call | tf_op jit(solution)/shard_map/jit(_solve_triangular)/triangular_solve | solution.py:759
  379.1 11.9 %custom-call.18 = f32[128,128]{1,0:T(8,128)S(1)} custom-call(f32[128,128]{1,0:T(8,128)S(1)} %convolution_subtract_fusion.6), custom_call_target="Cholesky" | custom-call | tf_op jit(solution)/shard_map/cholesky/custom-call.1 | solution.py:758
  392.3 9.8 %custom-call.19 = f32[1,128,128]{1,2,0:T(8,128)S(1)} custom-call(f32[1,128,128]{2,1,0:T(8,128)S(1)} %fusion.17), custom_call_target="InvertDiagBlocksLowerTriangular" | custom-call | tf_op jit(solution)/shard_map/jit(_solve_triangular)/triangular_solve | solution.py:759
  406.7 73.5 %project.1 = (f32[896,512]{1,0:T(8,128)}, bf16[8192,512]{1,0:T(8,128)(2,1)}) custom-call(f32[896,8192]{1,0:T(8,128)} %acc.5, bf16[256,512]{1,0:T(8,128)(2,1)} %copy.11.basis_ref, bf16[512,256]{1,0:T(8,128)(2,1)} %get-tuple-element.16.turned_ref, bf16[896,1024]{1,0:T(8,128)(2,1)} %grads_ref.5, bf16[256,1024]{1,0:T(8,128)(2,1)} %acts_ref.5), custom_call_target="tpu_custom_call" | custom-call | tf_op jit(solution)/shard_map/project/pallas_call | solution.py:724
  480.2 4.5 fusion
  484.8 18.2 %convolution_multiply_fusion = f32[896,8192]{1,0:T(8,128)} fusion(bf16[8192,512]{1,0:T(8,128)(2,1)} %get-tuple-element.9, f32[896,512]{1,0:T(8,128)S(1)} %get-tuple-element.14, f32[896,512]{1,0:T(8,128)} %get-tuple-element.15), kind=kOutput, calls=%fused_computation | convolution fusion | flops 7525826560 | bytes 41418752 | tf_op jit(solution)/shard_map/dot_general | solution.py:30
  (40 shorter events, 13.4 us)
Async XLA Ops:
  326.2 76.2 %copy-start = (f32[512,256]{1,0:T(8,128)S(1)}, f32[512,256]{1,0:T(8,128)}, u32[]{:S(2)}) copy-start(f32[512,256]{1,0:T(8,128)} %power_scatter.1) | copy-start | bytes 1572868
  484.8 18.2 %copy-start.1 = (f32[896,512]{1,0:T(8,128)}, f32[896,512]{1,0:T(8,128)S(1)}, u32[]{:S(2)}) copy-start(f32[896,512]{1,0:T(8,128)S(1)} %get-tuple-element.14) | copy-start | bytes 5505028

commit v3 on v2

--- a/solution.py
+++ b/solution.py
@@ -24,6 +24,8 @@
 VMEM = pl.BlockSpec(memory_space=pltpu.VMEM)
 DMA = pltpu.SemaphoreType.DMA
 vmem_bytes = 63 * 2**20
+image_ticks = (1, 0, 2, 2, 1, 1)
+power_lag, power_gap, power_ticks = 7, 4, (1, 3, 5, 7, 9, 11, 13, 15, 16)
 
 
 def mul(left, right, dims, precision=None):
@@ -51,13 +53,16 @@
         self.z, self.k = c // 2, c % 2
         self.c = c
         self.partner = (self.r, self.z * 2 + 1 - self.k)
+        n = self.chips
+        self.offsets = sorted(range(1, n), key=lambda d: -min(d, n - d))
 
     def flip(self, bit):
         return self.r + bit * (1 - 2 * ((self.r // bit) % 2))
 
-    def peer_row(self, s):
+    def peer_row(self, s, k=None):
+        k = self.k if k is None else k
         low, high_bit = 2**s, 2 ** (self.stages - 1 - s)
-        return (1 - self.k) * self.flip(low) + self.k * self.flip(high_bit)
+        return (1 - k) * self.flip(low) + k * self.flip(high_bit)
 
     def peer(self, s):
         return (self.peer_row(s), self.c)
@@ -65,15 +70,16 @@
     def count(self, s):
         return 2 ** (self.stages - 1 - s)
 
-    def block(self, s, j, base):
+    def block(self, s, j, base, k=None):
+        k = self.k if k is None else k
         n = self.count(s)
         first = base % 2 ** (s + 1) + j * 2 ** (s + 1)
         second = (base // n) * n + j
-        return (1 - self.k) * first + self.k * second
-
-    def chip(self, w):
-        n = self.chips
-        return (self.z + 1 + w) % n, (self.z + n - 1 - w) % n
+        return (1 - k) * first + k * second
+
+    def chip(self, w, far_first=False):
+        n, step = self.chips, self.offsets[w] if far_first else w + 1
+        return (self.z + step) % n, (self.z + n - step) % n
 
     def chip_device(self, z):
         return (self.r, z * 2 + self.k)
@@ -215,6 +221,75 @@
             copy.wait_send()
 
 
+class ChipsFirst(AllReduce):
+    def __init__(self, grid, *refs):
+        super().__init__(grid, *refs)
+        self.chunk = self.half // grid.chips
+        self.unit = self.chunk // grid.rows
+        self.phases = (
+            [self.pair_out, self.chips_out]
+            + [functools.partial(self.halve, s) for s in range(grid.stages)]
+            + [functools.partial(self.double, s) for s in reversed(range(grid.stages))]
+            + [self.chips_back, self.pair_back, self.finish]
+        )
+
+    @staticmethod
+    def scratch(rows, width, grid_rows, chips):
+        shapes = AllReduce.scratch(rows, width, grid_rows, chips)
+        half = rows // 2
+        unit = half // (chips * grid_rows)
+        shapes[3] = pltpu.VMEM((grid_rows - 1, unit, width), f32)
+        shapes[4] = pltpu.VMEM((chips - 1, half // chips, width), f32)
+        return shapes
+
+    def rows_of(self, r):
+        at = ((self.g.k * self.g.chips + self.g.z) * self.g.rows + r) * self.unit
+        return pl.ds(pl.multiple_of(at, self.unit), self.unit)
+
+    def chunk_of(self, z):
+        at = (self.g.k * self.g.chips + z) * self.chunk
+        return pl.ds(pl.multiple_of(at, self.chunk), self.chunk)
+
+    def chips_out(self):
+        g = self.g
+        self.landed()
+        mine = pl.ds(pl.multiple_of(g.k * self.half, self.half), self.half)
+        self.part[mine] += self.half_in[...]
+        for w in range(g.chips - 1):
+            z = g.chip(w)[0]
+            self.start(self.part.at[self.chunk_of(z)], self.chip_in.at[w], g.chip_device(z))
+
+    def halve(self, s):
+        g = self.g
+        self.landed()
+        if s == 0:
+            own = self.chunk_of(g.z)
+            total = self.part[own]
+            for w in range(g.chips - 1):
+                total = total + self.chip_in[w]
+            self.part[own] = total
+        else:
+            self.take(s - 1)
+        for j in range(g.count(s)):
+            rows = self.rows_of(g.block(s, j, g.peer_row(s)))
+            self.start(self.part.at[rows], self.stage_in.at[self.stage_base(s) + j], g.peer(s))
+
+    def double(self, s):
+        g = self.g
+        if s == g.stages - 1:
+            self.landed()
+            self.take(s)
+            self.full[self.rows_of(g.r)] = self.part[self.rows_of(g.r)]
+        super().double(s)
+
+    def chips_back(self):
+        g = self.g
+        self.landed()
+        own = self.chunk_of(g.z)
+        for w in range(g.chips - 1):
+            self.start(self.full.at[own], self.full.at[own], g.chip_device(g.chip(w)[0]))
+
+
 def reduce_kernel(rows, cols, part_ref, out_ref, *scratch):
     grid = Grid(rows, cols)
     grid.greet()
@@ -251,21 +326,27 @@
     rank = out_ref.shape[0]
     chips, stages = g.chips, g.stages
 
+    half = g.count(0)
+
     def chip_of(w):
-        return g.chip(w)[0]
-
-    def fetch(w, rp, kind):
+        return g.chip(w, True)[0] if w < chips - 1 else g.z
+
+    def block_of(t, kind=1):
+        w, i = t // rows, t % rows
         core = (1 - g.k) if kind == 0 else g.k
-        at = ((rp * chips + (g.z + 1 + w) % chips) * 2 + core) * blk
+        return w, g.block(0, i % half, g.peer_row(0, core) if i < half else g.r, core)
+
+    def fetch(t, kind):
+        w, rp = block_of(t, kind)
+        core = (1 - g.k) if kind == 0 else g.k
+        at = ((rp * chips + chip_of(w)) * 2 + core) * blk
         columns = pl.ds(pl.multiple_of(at, blk), blk)
-        slot = (w * rows + rp) % 2
-        return pltpu.make_async_copy(
-            acc.at[:, columns], tiles.at[kind * 2 + slot], tile_sem.at[kind * 2 + slot]
-        )
-
-    for rp in range(2):
-        fetch(0, rp, 0).start()
-        fetch(0, rp, 1).start()
+        slot = kind * 2 + t % 2
+        return pltpu.make_async_copy(acc.at[:, columns], tiles.at[slot], tile_sem.at[slot])
+
+    for t in range(2):
+        fetch(t, 0).start()
+        fetch(t, 1).start()
     g.greet()
 
     part, full, *rest = reduce_scratch
@@ -302,62 +383,59 @@
             g.chip_device(chip_of(w)),
         )
 
-    def compute(w):
-        def step(rp, carry):
-            i = w * rows + rp
-            slot = i % 2
-            for kind, store in ((0, theirs), (1, mine)):
-                fetch(w, rp, kind).wait()
-                store[i] = product(kind * 2 + slot)
-                if kind == 0:
-                    pair_copy(w, rp).start()
-
-                @pl.when(i + 2 < chips * rows)
-                def _():
-                    fetch((i + 2) // rows, (i + 2) % rows, kind).start()
-            return carry
-
-        lax.fori_loop(0, rows, step, 0)
-
-    def add(index, value_ref, at):
-        mine[index] += value_ref[at]
+    def compute(t):
+        for kind, store in ((0, theirs), (1, mine)):
+            w, rp = block_of(t, kind)
+            fetch(t, kind).wait()
+            store[w * rows + rp] = product(kind * 2 + t % 2)
+            if kind == 0:
+                pair_copy(w, rp).start()
+            if t + 2 < chips * rows:
+                fetch(t + 2, kind).start()
+
+    def pair(t):
+        w, rp = block_of(t)
+        pair_copy(w, rp).wait_recv()
+        mine[w * rows + rp] += pair_in[w * rows + rp]
+        if t % rows < half:
+            stage_copy(w, 0, t % rows).start()
 
     def halve(w, s):
-        if s == 0:
-            for base, send in ((g.peer_row(0), True), (g.r, False)):
-                for j in range(g.count(0)):
-                    rp = g.block(0, j, base)
-                    pair_copy(w, rp).wait_recv()
-                    add(w * rows + rp, pair_in, w * rows + rp)
-                    if send:
-                        stage_copy(w, 0, j).start()
-            return
         for j in range(g.count(s - 1)):
             i = w * (rows - 1) + rows - 2 ** (stages - s + 1) + j
             stage_copy(w, s - 1, j).wait_recv()
-            add(w * rows + g.block(s - 1, j, g.r), stage_in, i)
+            mine[w * rows + g.block(s - 1, j, g.r)] += stage_in[i]
         for j in range(g.count(s)):
             stage_copy(w, s, j).start()
 
     def leave(w):
         i = w * (rows - 1) + rows - 2
         stage_copy(w, stages - 1, 0).wait_recv()
-        add(w * rows + g.r, stage_in, i)
+        mine[w * rows + g.r] += stage_in[i]
         if w < chips - 1:
             chip_copy(w).start()
 
-    for at in range(chips + stages + 1):
-        if at < chips:
-            compute(at)
-        for later in range(1, stages + 1):
-            w = at - later
-            if 0 <= w < chips:
-                tick()
-                halve(w, later - 1)
-        w = at - stages - 1
-        if 0 <= w < chips:
+    steps = chips * rows
+    lag, gap, ticks = power_lag, power_gap, power_ticks
+    later = {}
+    for w in range(chips):
+        for s in range(1, stages):
+            later.setdefault(min(lag + gap * w + 3 * (s - 1), steps + 2 * w + s), []).append(
+                functools.partial(halve, w, s)
+            )
+    for w in range(chips):
+        later.setdefault(min(lag + gap * w + gap, steps + 2 * w + 3), []).append(
+            functools.partial(leave, w)
+        )
+    for t in range(max(max(later), steps) + 1):
+        if t in ticks:
             tick()
-            leave(w)
+        if t < steps:
+            compute(t)
+        if 0 < t <= steps:
+            pair(t - 1)
+        for event in later.get(t, ()):
+            event()
     for phase in phases:
         phase()
     upper, lower = split(full[...])
@@ -463,7 +541,7 @@
     part, full, *rest = reduce_scratch
     upper, lower = split(turned)
     part[...] = mul(upper, acts_ref[...], rows_cols) + mul(lower, acts_ref[...], rows_cols)
-    tokens = AllReduce(g, part, full, *rest)
+    tokens = ChipsFirst(g, part, full, *rest)
     small = Interleaved(tokens.phases)
     small.tick()
 
@@ -540,7 +618,7 @@
     done = 0
     lag = stages
     for at in range(pieces + lag):
-        small.tick(2)
+        small.tick(image_ticks[at] if at < len(image_ticks) else 1)
         for late in range(stages):
             i = at - late
             if 0 <= i < pieces:
@@ -591,7 +669,7 @@
             DMA((4,)),
             DMA((2, pieces * rows)),
             DMA((2, pieces * (rows - 1))),
-            *AllReduce.scratch(rank, acts.shape[1], rows, cols // 2),
+            *ChipsFirst.scratch(rank, acts.shape[1], rows, cols // 2),
         ],
         compiler_params=pltpu.CompilerParams(
             collective_id=collective_id, has_side_effects=True, vmem_limit_bytes=vmem_bytes
@@ -646,9 +724,8 @@
     def chip_copy(w, z):
         at = ((g.r * chips + z) * 2 + g.k) * blk
         ref = full_ref.at[pl.ds(pl.multiple_of(at, blk), blk)]
-        return remote(
-            ref, ref, chip_sems.at[0, w], chip_sems.at[1, w], g.chip_device(g.chip(w)[0])
-        )
+        device = g.chip_device(g.chip(w)[0])
+        return remote(ref, ref, chip_sems.at[0, w], chip_sems.at[1, w], device)
 
     def enter(w):
         if w > 0:
@@ -742,6 +819,97 @@
         ),
         name="project",
     )(accumulated, basis, turned, grads, acts)
+
+
+def orthogonal_kernel(rows, cols, step, power_ref, out_ref, turned_ref, gram, rest, *reduce_scratch):
+    g = Grid(rows, cols)
+    g.greet()
+    part, full, *others = reduce_scratch
+    rank = gram.shape[0]
+    count = rank // step
+    product = mul(power_ref[...], power_ref[...], cols_cols, highest)
+    across = part.shape[1] // step
+    lower_blocks = [(i, j) for i in range(count) for j in range(i + 1)]
+
+    def cut(n):
+        return slice(n * step, (n + 1) * step)
+
+    for n in range(count * across):
+        i, j = lower_blocks[n] if n < len(lower_blocks) else (0, 0)
+        part[cut(n // across), cut(n % across)] = product[cut(i), cut(j)]
+    total = AllReduce(g, part, full, *others)
+    for phase in total.phases:
+        phase()
+    rest[...] = power_ref[...]
+    for n, (i, j) in enumerate(lower_blocks):
+        gram[cut(i), cut(j)] = full[cut(n // across), cut(n % across)]
+        if i > j:
+            gram[cut(j), cut(i)] = jnp.zeros((step, step), f32)
+    lanes = lax.broadcasted_iota(jnp.int32, (step, step), 1)
+    lines = lax.broadcasted_iota(jnp.int32, (step, step), 0)
+
+    def eliminate(j, carry):
+        at = pl.ds(pl.multiple_of(j * step, step), step)
+        left = gram[at, at]
+        right = (lanes == lines).astype(f32)
+        left_parts = [left[8 * i : 8 * i + 8] for i in range(step // 8)]
+        right_parts = [right[8 * i : 8 * i + 8] for i in range(step // 8)]
+        eights = lax.broadcasted_iota(jnp.int32, (8, step), 0)
+        for n in range(step):
+            q, o = n // 8, n % 8
+            pivot_row = left_parts[q][o : o + 1]
+            pivot_right = right_parts[q][o : o + 1]
+            scale = 1.0 / pivot_row[:, n : n + 1]
+            pivot_row = pivot_row * scale
+            pivot_right = pivot_right * scale
+            for i in range(q, step // 8):
+                if i == q:
+                    if o == 7:
+                        continue
+                    column = jnp.where(eights > o, left_parts[i][:, n : n + 1], 0.0)
+                else:
+                    column = left_parts[i][:, n : n + 1]
+                left_parts[i] = left_parts[i] - column * pivot_row
+                right_parts[i] = right_parts[i] - column * pivot_right
+        left = jnp.concatenate(left_parts, axis=0)
+        right = jnp.concatenate(right_parts, axis=0)
+        diagonal = jnp.sum(jnp.where(lanes == lines, left, 0.0), axis=1, keepdims=True)
+        inverse = right * lax.rsqrt(diagonal)
+        panel = mul(gram[:, at], inverse, cols_cols, highest)
+        below = lax.broadcasted_iota(jnp.int32, panel.shape, 0) >= (j + 1) * step
+        panel = jnp.where(below, panel, 0.0)
+        gram[...] -= mul(panel, panel, cols_cols, highest)
+        solved = mul(inverse, rest[at], rows_cols, highest)
+        rest[...] -= mul(panel, solved, rows_cols, highest)
+        turned_ref[at] = solved.astype(bf16)
+        return carry
+
+    lax.fori_loop(0, rank // step, eliminate, 0)
+    out_ref[...] = turned_ref[...].astype(f32).T.astype(bf16)
+    total.drain()
+
+
+def orthogonal(power_turned, rows, cols, collective_id):
+    rank, blk = power_turned.shape
+    blocks = rank // 128
+    return pl.pallas_call(
+        functools.partial(orthogonal_kernel, rows, cols, 128),
+        out_shape=(
+            jax.ShapeDtypeStruct((blk, rank), bf16),
+            jax.ShapeDtypeStruct((rank, blk), bf16),
+        ),
+        in_specs=[VMEM],
+        out_specs=(VMEM, VMEM),
+        scratch_shapes=[
+            pltpu.VMEM((rank, rank), f32),
+            pltpu.VMEM((rank, blk), f32),
+            *AllReduce.scratch(rank, 128 * -(-blocks * (blocks + 1) // (2 * blocks)), rows, cols // 2),
+        ],
+        compiler_params=pltpu.CompilerParams(
+            collective_id=collective_id, has_side_effects=True, vmem_limit_bytes=vmem_bytes
+        ),
+        name="orthogonal",
+    )(power_turned)
 
 
 def solve_lower(gram_matrix, right):
@@ -815,11 +983,7 @@
     common = (out_grads, activations, rows, cols)
     pair = image_pair(accumulated, seed_basis, *common, 1)
     power_turned = power_scatter(accumulated, pair, *common, 2)
-    gram_matrix = all_reduce(
-        mul(power_turned, power_turned, cols_cols, highest), rows, cols, 3
-    )
-    turned = solve_lower(gram_matrix, power_turned).astype(bf16)
-    basis_rows = turned.T
+    basis_rows, turned = orthogonal(power_turned, rows, cols, 3)
     projected, full_basis = project(accumulated, basis_rows, turned, *common, 4)
     return (basis_rows, *finish(moment_first, moment_second, projected, full_basis))
 
@@ -831,6 +995,7 @@
         rank = others[2].shape[1]
         fits = rows & (rows - 1) == 0 and rows > 1 and cols % 2 == 0 and cols > 2
         fits = fits and activations.shape[0] % 128 == 0 and rank % (8 * rows * cols) == 0
+        fits = fits and rank % 128 == 0
         if fits:
             return body(rows, cols, activations, *others)
         return plain_body(activations, *others)

time: 513 us -> 411 us (0.80)
  other arithmetic: 97 us -> 4.53 us
  matrix products: 37.1 us -> 18.3 us
  Pallas kernels: 366 us -> 382 us
    another operation x20 -> x0, other arithmetic: 91.8 us -> none  [the longest x12 49.9 us: solve_lower(): factor = lax.linalg.cholesky(trailing[j, j], symmetrize_input=False)]
    pallas_call x1, Pallas kernels: 35.3 us -> 87.3 us  [orthogonal(): pl.pallas_call(functools.partial(orthogonal_kernel, rows, cols, 128), out...]
    pallas_call x1, Pallas kernels: 141 us -> 110 us  [power_scatter(): pl.pallas_call(functools.partial(power_kernel, rows, cols), out_shape=jax...]
    dot_general x28 -> x1, matrix products: 36 us -> 18.3 us  [mul(): lax.dot_general(left, right, (dims, ((), ())), precision=precision, prefe...]
    pallas_call x1, Pallas kernels: 117 us -> 110 us  [image_pair(): pl.pallas_call(functools.partial(image_kernel, rows, cols), out_shape=jax...]
where the time goes in v3:
time: 411 us; the launch traced here: 406 us
  Pallas kernels  382 us (93%)
  matrix products  18.3 us (4%)
  other arithmetic  4.53 us (1%)
    pallas_call x1, Pallas kernels, image_pair(): pl.pallas_call(functools.partial(image_kernel, rows, cols), out_shape=jax...  110 us
    pallas_call x1, Pallas kernels, power_scatter(): pl.pallas_call(functools.partial(power_kernel, rows, cols), out_shape=jax...  110 us
    pallas_call x1, Pallas kernels, orthogonal(): pl.pallas_call(functools.partial(orthogonal_kernel, rows, cols, 128), out...  87.3 us
    pallas_call x1, Pallas kernels, project(): pl.pallas_call(functools.partial(project_kernel, rows, cols), out_shape=(...  75.1 us
    dot_general x1, matrix products, mul(): lax.dot_general(left, right, (dims, ((), ())), precision=precision, prefe...  18.3 us

profile of v3, /device:TPU:25, one launch (start us, length us, event | category | flops | bytes accessed | tf_op | source)
XLA Modules:
  0.0 406.5 jit_solution(14000995935079549814)
XLA Ops:
  0.6 109.7 %image_pair.1.pair_ref = bf16[1024,896]{1,0:T(8,128)(2,1)} custom-call(f32[896,8192]{1,0:T(8,128)} %acc.5, f32[2048,512]{1,0:T(8,128)} %seed_ref.1, bf16[896,1024]{1,0:T(8,128)(2,1)} %grads_ref.5, bf16[256,1024]{1,0:T(8,128)(2,1)} %acts_ref.5), custom_call_target="tpu_custom_call" | custom-call | tf_op jit(solution)/shard_map/image_pair/pallas_call | solution.py:660
  110.4 109.6 %power_scatter.1.power_ref = f32[512,256]{1,0:T(8,128)} custom-call(f32[896,8192]{1,0:T(8,128)} %acc.5, bf16[1024,896]{1,0:T(8,128)(2,1)} %image_pair.1.pair_ref, bf16[896,1024]{1,0:T(8,128)(2,1)} %grads_ref.5, bf16[256,1024]{1,0:T(8,128)(2,1)} %acts_ref.5), custom_call_target="tpu_custom_call" | custom-call | tf_op jit(solution)/shard_map/power_scatter/pallas_call | solution.py:469
  220.0 87.3 %orthogonal.1 = (bf16[256,512]{1,0:T(8,128)(2,1)}, bf16[512,256]{1,0:T(8,128)(2,1)}) custom-call(f32[512,256]{1,0:T(8,128)} %power_scatter.1.power_ref), custom_call_target="tpu_custom_call" | custom-call | tf_op jit(solution)/shard_map/orthogonal/pallas_call | solution.py:895
  307.3 75.1 %project.1 = (f32[896,512]{1,0:T(8,128)}, bf16[8192,512]{1,0:T(8,128)(2,1)}) custom-call(f32[896,8192]{1,0:T(8,128)} %acc.5, bf16[256,512]{1,0:T(8,128)(2,1)} %get-tuple-element.18.basis_ref, bf16[512,256]{1,0:T(8,128)(2,1)} %get-tuple-element.9.turned_ref, bf16[896,1024]{1,0:T(8,128)(2,1)} %grads_ref.5, bf16[256,1024]{1,0:T(8,128)(2,1)} %acts_ref.5), custom_call_target="tpu_custom_call" | custom-call | tf_op jit(solution)/shard_map/project/pallas_call | solution.py:801
  382.4 4.5 %fusion = (f32[896,512]{1,0:T(8,128)S(1)}, f32[896,512]{1,0:T(8,128)}) fusion(f32[896,512]{1,0:T(8,128)} %get-tuple-element.10, f32[896,512]{1,0:T(8,128)} %param.11, f32[896,512]{1,0:T(8,128)} %param.10), kind=kLoop, calls=%fused_computation.2 | loop fusion | flops 3211264 | bytes 9175040 | tf_op jit(solution)/shard_map/add | solution.py:943
  387.0 0.0 copy-start
  387.0 0.0 copy-start.1
  387.0 18.3 %convolution_multiply_fusion = f32[896,8192]{1,0:T(8,128)} fusion(bf16[8192,512]{1,0:T(8,128)(2,1)} %get-tuple-element.11, f32[896,512]{1,0:T(8,128)S(1)} %get-tuple-element.20, f32[896,512]{1,0:T(8,128)} %get-tuple-element.19), kind=kOutput, calls=%fused_computation | convolution fusion | flops 7525826560 | bytes 41418752 | tf_op jit(solution)/shard_map/dot_general | solution.py:32
  405.3 0.0 copy-done
  405.3 0.0 copy-done.1
  405.3 0.7 copy.11
Async XLA Ops:
  387.0 18.3 %copy-start = (f32[896,512]{1,0:T(8,128)}, f32[896,512]{1,0:T(8,128)S(1)}, u32[]{:S(2)}) copy-start(f32[896,512]{1,0:T(8,128)S(1)} %get-tuple-element.20) | copy-start | bytes 5505028
  387.0 18.3 %copy-start.1 = (bf16[256,512]{1,0:T(8,128)(2,1)S(1)}, bf16[256,512]{1,0:T(8,128)(2,1)}, u32[]{:S(2)}) copy-start(bf16[256,512]{1,0:T(8,128)(2,1)} %get-tuple-element.18.basis_ref) | copy-start | bytes 786436

commit v4 on v3

--- a/solution.py
+++ b/solution.py
@@ -24,6 +24,7 @@
 VMEM = pl.BlockSpec(memory_space=pltpu.VMEM)
 DMA = pltpu.SemaphoreType.DMA
 vmem_bytes = 63 * 2**20
+image_gather = 4
 image_ticks = (1, 0, 2, 2, 1, 1)
 power_lag, power_gap, power_ticks = 7, 4, (1, 3, 5, 7, 9, 11, 13, 15, 16)
 
@@ -349,20 +350,6 @@
         fetch(t, 1).start()
     g.greet()
 
-    part, full, *rest = reduce_scratch
-    part[...] = mul(pair_ref[:rank], grads_ref[...], rows_cols) + mul(
-        pair_ref[rank:], grads_ref[...], rows_cols
-    )
-    tokens = AllReduce(g, part, full, *rest)
-    phases = iter(tokens.phases)
-
-    def tick():
-        phase = next(phases, None)
-        if phase is not None:
-            phase()
-
-    tick()
-
     def product(slot):
         upper, lower = split(tiles[slot])
         both = mul(pair_ref[...], upper, rows_cols)
@@ -415,6 +402,20 @@
         if w < chips - 1:
             chip_copy(w).start()
 
+    part, full, *rest = reduce_scratch
+
+    part[...] = mul(pair_ref[:rank], grads_ref[...], rows_cols) + mul(
+        pair_ref[rank:], grads_ref[...], rows_cols
+    )
+    tokens = AllReduce(g, part, full, *rest)
+    phases = iter(tokens.phases)
+
+    def tick():
+        phase = next(phases, None)
+        if phase is not None:
+            phase()
+
+    tick()
     steps = chips * rows
     lag, gap, ticks = power_lag, power_gap, power_ticks
     later = {}
@@ -506,7 +507,7 @@
 
 def image_kernel(
     rows, cols, acc, seed_ref, grads_ref, acts_ref, out_ref,
-    tiles, image, seeds, tile_sem, pair_sems, stage_sems, *reduce_scratch,
+    tiles, image, seeds, tile_sem, pair_sems, stage_sems, share_sems, *reduce_scratch,
 ):
     g = Grid(rows, cols)
     stages = g.stages
@@ -526,7 +527,7 @@
         u = t - 2 * pieces
         wave = u // (2 * (rows - 1))
         inner = u % (2 * (rows - 1))
-        other = piece((g.r + 1 + inner // 2) % rows, inner % 2, wave)
+        other = piece((g.r + 1 + inner // 2) % rows, inner % 2, (wave + 1) % pieces)
         own = piece(g.r, t // pieces, t % pieces)
         return jnp.where(t < 2 * pieces, own, other)
 
@@ -536,6 +537,95 @@
         fetch(order(t), t).start()
     g.greet()
 
+    def spread(q):
+        at = pl.ds(pl.multiple_of(q * blk, blk), blk)
+        upper, lower = split(seed_ref[at])
+        target = g.r * 2 * pieces + q
+        seeds[target, 0] = upper
+        seeds[target, 1] = lower
+
+    share = blk // g.chips
+
+    def shared(p, z):
+        return seeds.at[p, :, pl.ds(pl.multiple_of(z * share, share), share)]
+
+    def share_copy(s, j, w, z):
+        at = (rows - 2 ** (stages - s) + j) * (g.chips - 1) + w
+        ref = shared(piece(g.block(s, j, g.peer_row(s)), g.k, 0), z)
+        device = g.chip_device(g.chip(w)[0])
+        return remote(ref, ref, share_sems.at[0, at], share_sems.at[1, at], device)
+
+    def pair_copy(rp, i):
+        p = piece(rp, g.k, i)
+        at = i * rows + rp
+        return remote(seeds.at[p], seeds.at[p], pair_sems.at[0, at], pair_sems.at[1, at], g.partner)
+
+    def pair_wait(rp, i):
+        at = i * rows + rp
+        p = piece(rp, 1 - g.k, i)
+        remote(seeds.at[p], seeds.at[p], pair_sems.at[0, at], pair_sems.at[1, at], g.partner).wait_recv()
+
+    def stage_copy(i, s, j, base):
+        at = i * (rows - 1) + rows - 2 ** (stages - s) + j
+        p = piece(g.block(s, j, base), g.k, i)
+        ref = seeds.at[p] if i else shared(p, g.z)
+        return remote(ref, ref, stage_sems.at[0, at], stage_sems.at[1, at], g.peer(s))
+
+    def send(i, s):
+        for j in range(g.count(s)):
+            stage_copy(i, s, j, g.r).start()
+
+    def land(i, s):
+        for j in range(g.count(s)):
+            stage_copy(i, s, j, g.peer_row(s)).wait_recv()
+            if i:
+                pair_copy(g.block(s, j, g.peer_row(s)), i).start()
+            else:
+                for w in range(g.chips - 1):
+                    share_copy(s, j, w, g.z).start()
+
+    def gather():
+        for s in reversed(range(stages)):
+            for j in range(g.count(s)):
+                for w in range(g.chips - 1):
+                    share_copy(s, j, w, g.chip(w)[1]).wait_recv()
+                pair_copy(g.block(s, j, g.peer_row(s)), 0).start()
+
+    def compute(t):
+        slot = t % depth
+        p = order(t)
+        fetch(p, slot).wait()
+
+        @pl.when(t + depth - 1 < count)
+        def _():
+            fetch(order(t + depth - 1), (t + depth - 1) % depth).start()
+
+        upper, lower = split(tiles[slot])
+        image[...] += (
+            mul(upper, seeds[p, 0], rows_cols)
+            + mul(lower, seeds[p, 0], rows_cols)
+            + mul(upper, seeds[p, 1], rows_cols)
+        )
+
+    def own_step(t, carry):
+        compute(t)
+        return carry
+
+    def other_step(t, carry):
+        inner = (t - 2 * pieces) % (2 * (rows - 1))
+        wave = (t - 2 * pieces) // (2 * (rows - 1))
+        rp = (g.r + 1 + inner // 2) % rows
+
+        @pl.when(inner % 2 == 1 - g.k)
+        def _():
+            pair_wait(rp, (wave + 1) % pieces)
+
+        compute(t)
+        return carry
+
+    for i in range(pieces):
+        spread(g.k * pieces + i)
+        send(i, stages - 1)
     own = pl.ds(pl.multiple_of(g.c * tokens_rows, tokens_rows), tokens_rows)
     turned = seed_ref[own].T
     part, full, *rest = reduce_scratch
@@ -545,75 +635,12 @@
     small = Interleaved(tokens.phases)
     small.tick()
 
-    def spread(q, carry):
-        at = pl.ds(pl.multiple_of(q * blk, blk), blk)
-        upper, lower = split(seed_ref[at])
-        target = g.r * 2 * pieces + q
-        seeds[target, 0] = upper
-        seeds[target, 1] = lower
+    def spread_other(i, carry):
+        spread((1 - g.k) * pieces + i)
         return carry
 
-    lax.fori_loop(0, 2 * pieces, spread, 0)
-
-    def pair_copy(rp, i):
-        p = piece(rp, g.k, i)
-        at = i * rows + rp
-        return remote(seeds.at[p], seeds.at[p], pair_sems.at[0, at], pair_sems.at[1, at], g.partner)
-
-    def pair_wait(rp, i):
-        at = i * rows + rp
-        p = piece(rp, 1 - g.k, i)
-        remote(seeds.at[p], seeds.at[p], pair_sems.at[0, at], pair_sems.at[1, at], g.partner).wait_recv()
-
-    def stage_copy(i, s, j, base):
-        at = i * (rows - 1) + rows - 2 ** (stages - s) + j
-        p = piece(g.block(s, j, base), g.k, i)
-        return remote(seeds.at[p], seeds.at[p], stage_sems.at[0, at], stage_sems.at[1, at], g.peer(s))
-
-    def send(i, s):
-        for j in range(g.count(s)):
-            stage_copy(i, s, j, g.r).start()
-
-    def land(i, s):
-        for j in range(g.count(s)):
-            stage_copy(i, s, j, g.peer_row(s)).wait_recv()
-            pair_copy(g.block(s, j, g.peer_row(s)), i).start()
-
-    def compute(t):
-        slot = t % depth
-        p = order(t)
-        fetch(p, slot).wait()
-
-        @pl.when(t + depth - 1 < count)
-        def _():
-            fetch(order(t + depth - 1), (t + depth - 1) % depth).start()
-
-        upper, lower = split(tiles[slot])
-        image[...] += (
-            mul(upper, seeds[p, 0], rows_cols)
-            + mul(lower, seeds[p, 0], rows_cols)
-            + mul(upper, seeds[p, 1], rows_cols)
-        )
-
-    def own_step(t, carry):
-        compute(t)
-        return carry
-
-    def other_step(t, carry):
-        inner = (t - 2 * pieces) % (2 * (rows - 1))
-        wave = (t - 2 * pieces) // (2 * (rows - 1))
-        rp = (g.r + 1 + inner // 2) % rows
-
-        @pl.when(inner % 2 == 1 - g.k)
-        def _():
-            pair_wait(rp, wave)
-
-        compute(t)
-        return carry
-
+    lax.fori_loop(0, pieces, spread_other, 0)
     image[...] = jnp.zeros_like(image)
-    for i in range(pieces):
-        send(i, stages - 1)
     first = 2 * pieces // (stages + 1)
     done = 0
     lag = stages
@@ -626,6 +653,8 @@
                 land(i, s)
                 if s > 0:
                     send(i, s - 1)
+        if at == image_gather:
+            gather()
         if done < 2 * pieces:
             stop = min(2 * pieces, done + first)
             lax.fori_loop(done, stop, own_step, 0)
@@ -649,6 +678,10 @@
             for j in range(g.count(s)):
                 stage_copy(i, s, j, g.r).wait_send()
                 pair_copy(g.block(s, j, g.peer_row(s)), i).wait_send()
+    for s in range(stages):
+        for j in range(g.count(s)):
+            for w in range(g.chips - 1):
+                share_copy(s, j, w, g.z).wait_send()
 
 
 def image_pair(accumulated, seed, grads, acts, rows, cols, collective_id):
@@ -669,6 +702,7 @@
             DMA((4,)),
             DMA((2, pieces * rows)),
             DMA((2, pieces * (rows - 1))),
+            DMA((2, (cols // 2 - 1) * (rows - 1))),
             *ChipsFirst.scratch(rank, acts.shape[1], rows, cols // 2),
         ],
         compiler_params=pltpu.CompilerParams(
@@ -845,36 +879,65 @@
         gram[cut(i), cut(j)] = full[cut(n // across), cut(n % across)]
         if i > j:
             gram[cut(j), cut(i)] = jnp.zeros((step, step), f32)
-    lanes = lax.broadcasted_iota(jnp.int32, (step, step), 1)
-    lines = lax.broadcasted_iota(jnp.int32, (step, step), 0)
+    part_step = step // 2
+    lanes = lax.broadcasted_iota(jnp.int32, (part_step, part_step), 1)
+    lines = lax.broadcasted_iota(jnp.int32, (part_step, part_step), 0)
+    eights = lax.broadcasted_iota(jnp.int32, (8, step), 0)
+
+    def invert(block):
+        both = jnp.concatenate([block, (lanes == lines).astype(f32)], axis=1)
+        parts = [both[8 * i : 8 * i + 8] for i in range(part_step // 8)]
+        for n in range(0, part_step, 2):
+            q, o = n // 8, n % 8
+            wide = (8, step)
+            first = jnp.broadcast_to(parts[q][:, n : n + 1], wide)
+            second = jnp.broadcast_to(parts[q][:, n + 1 : n + 2], wide)
+            row_a = jnp.broadcast_to(parts[q][o : o + 1], wide)
+            row_b = jnp.broadcast_to(parts[q][o + 1 : o + 2], wide)
+            aa = jnp.broadcast_to(first[o : o + 1], wide)
+            ab = jnp.broadcast_to(first[o + 1 : o + 2], wide)
+            bb = jnp.broadcast_to(second[o + 1 : o + 2], wide)
+            scale = 1.0 / (aa * bb - ab * ab)
+            take_a = (row_a * bb - row_b * ab) * scale
+            take_b = (row_b * aa - row_a * ab) * scale
+            if o < 6:
+                later = eights > o + 1
+                parts[q] = (
+                    parts[q]
+                    - jnp.where(later, first, 0.0) * take_a
+                    - jnp.where(later, second, 0.0) * take_b
+                )
+            for i in range(q + 1, part_step // 8):
+                parts[i] = (
+                    parts[i]
+                    - parts[i][:, n : n + 1] * take_a
+                    - parts[i][:, n + 1 : n + 2] * take_b
+                )
+        both = jnp.concatenate(parts, axis=0)
+        left, right = both[:, :part_step], both[:, part_step:]
+        odd = lines % 2 == 1
+        diagonal = jnp.sum(jnp.where(lanes == lines, left, 0.0), axis=1, keepdims=True)
+        side = jnp.sum(
+            jnp.where(odd & (lanes == lines - 1), left, 0.0), axis=1, keepdims=True
+        )
+        diagonal = jnp.broadcast_to(diagonal, left.shape)
+        side = jnp.broadcast_to(side, left.shape)
+        ratio = jnp.where(odd, side / pltpu.roll(diagonal, 1, 0), 0.0)
+        right = right - ratio * pltpu.roll(right, 1, 0)
+        return right * lax.rsqrt(diagonal - ratio * side)
 
     def eliminate(j, carry):
         at = pl.ds(pl.multiple_of(j * step, step), step)
-        left = gram[at, at]
-        right = (lanes == lines).astype(f32)
-        left_parts = [left[8 * i : 8 * i + 8] for i in range(step // 8)]
-        right_parts = [right[8 * i : 8 * i + 8] for i in range(step // 8)]
-        eights = lax.broadcasted_iota(jnp.int32, (8, step), 0)
-        for n in range(step):
-            q, o = n // 8, n % 8
-            pivot_row = left_parts[q][o : o + 1]
-            pivot_right = right_parts[q][o : o + 1]
-            scale = 1.0 / pivot_row[:, n : n + 1]
-            pivot_row = pivot_row * scale
-            pivot_right = pivot_right * scale
-            for i in range(q, step // 8):
-                if i == q:
-                    if o == 7:
-                        continue
-                    column = jnp.where(eights > o, left_parts[i][:, n : n + 1], 0.0)
-                else:
-                    column = left_parts[i][:, n : n + 1]
-                left_parts[i] = left_parts[i] - column * pivot_row
-                right_parts[i] = right_parts[i] - column * pivot_right
-        left = jnp.concatenate(left_parts, axis=0)
-        right = jnp.concatenate(right_parts, axis=0)
-        diagonal = jnp.sum(jnp.where(lanes == lines, left, 0.0), axis=1, keepdims=True)
-        inverse = right * lax.rsqrt(diagonal)
+        block = gram[at, at]
+        first = invert(block[:part_step, :part_step])
+        link = mul(block[part_step:, :part_step], first, cols_cols, highest)
+        second = invert(block[part_step:, part_step:] - mul(link, link, cols_cols, highest))
+        below = -mul(second, mul(link, first, rows_cols, highest), rows_cols, highest)
+        above = jnp.zeros_like(below)
+        inverse = jnp.concatenate(
+            [jnp.concatenate([first, above], axis=1), jnp.concatenate([below, second], axis=1)],
+            axis=0,
+        )
         panel = mul(gram[:, at], inverse, cols_cols, highest)
         below = lax.broadcasted_iota(jnp.int32, panel.shape, 0) >= (j + 1) * step
         panel = jnp.where(below, panel, 0.0)
@@ -995,7 +1058,7 @@
         rank = others[2].shape[1]
         fits = rows & (rows - 1) == 0 and rows > 1 and cols % 2 == 0 and cols > 2
         fits = fits and activations.shape[0] % 128 == 0 and rank % (8 * rows * cols) == 0
-        fits = fits and rank % 128 == 0
+        fits = fits and rank % 128 == 0 and 256 % (16 * cols // 2) == 0
         if fits:
             return body(rows, cols, activations, *others)
         return plain_body(activations, *others)

time: 411 us -> 400 us (0.973)
  Pallas kernels: 382 us -> 370 us
    pallas_call x1, Pallas kernels: 110 us -> 103 us  [image_pair(): pl.pallas_call(functools.partial(image_kernel, rows, cols), out_shape=jax...]
    pallas_call x1, Pallas kernels: 87.3 us -> 82.8 us  [orthogonal(): pl.pallas_call(functools.partial(orthogonal_kernel, rows, cols, 128), out...]
where the time goes in v4:
time: 400 us; the launch traced here: 395 us
  Pallas kernels  370 us (92%)
  matrix products  18.3 us (5%)
  other arithmetic  4.53 us (1%)
    pallas_call x1, Pallas kernels, power_scatter(): pl.pallas_call(functools.partial(power_kernel, rows, cols), out_shape=jax...  111 us
    pallas_call x1, Pallas kernels, image_pair(): pl.pallas_call(functools.partial(image_kernel, rows, cols), out_shape=jax...  103 us
    pallas_call x1, Pallas kernels, orthogonal(): pl.pallas_call(functools.partial(orthogonal_kernel, rows, cols, 128), out...  82.8 us
    pallas_call x1, Pallas kernels, project(): pl.pallas_call(functools.partial(project_kernel, rows, cols), out_shape=(...  73.1 us
    dot_general x1, matrix products, mul(): lax.dot_general(left, right, (dims, ((), ())), precision=precision, prefe...  18.3 us

profile of v4, /device:TPU:25, one launch (start us, length us, event | category | flops | bytes accessed | tf_op | source)
XLA Modules:
  0.0 394.6 jit_solution(14182029689264317443)
XLA Ops:
  0.6 103.1 %image_pair.1.pair_ref = bf16[1024,896]{1,0:T(8,128)(2,1)} custom-call(f32[896,8192]{1,0:T(8,128)} %acc.5, f32[2048,512]{1,0:T(8,128)} %seed_ref.1, bf16[896,1024]{1,0:T(8,128)(2,1)} %grads_ref.5, bf16[256,1024]{1,0:T(8,128)(2,1)} %acts_ref.5), custom_call_target="tpu_custom_call" | custom-call | tf_op jit(solution)/shard_map/image_pair/pallas_call | solution.py:693
  103.7 110.9 %power_scatter.1.power_ref = f32[512,256]{1,0:T(8,128)} custom-call(f32[896,8192]{1,0:T(8,128)} %acc.5, bf16[1024,896]{1,0:T(8,128)(2,1)} %image_pair.1.pair_ref, bf16[896,1024]{1,0:T(8,128)(2,1)} %grads_ref.5, bf16[256,1024]{1,0:T(8,128)(2,1)} %acts_ref.5), custom_call_target="tpu_custom_call" | custom-call | tf_op jit(solution)/shard_map/power_scatter/pallas_call | solution.py:470
  214.7 82.8 %orthogonal.1 = (bf16[256,512]{1,0:T(8,128)(2,1)}, bf16[512,256]{1,0:T(8,128)(2,1)}) custom-call(f32[512,256]{1,0:T(8,128)} %power_scatter.1.power_ref), custom_call_target="tpu_custom_call" | custom-call | tf_op jit(solution)/shard_map/orthogonal/pallas_call | solution.py:958
  297.5 73.1 %project.1 = (f32[896,512]{1,0:T(8,128)}, bf16[8192,512]{1,0:T(8,128)(2,1)}) custom-call(f32[896,8192]{1,0:T(8,128)} %acc.5, bf16[256,512]{1,0:T(8,128)(2,1)} %get-tuple-element.18.basis_ref, bf16[512,256]{1,0:T(8,128)(2,1)} %get-tuple-element.9.turned_ref, bf16[896,1024]{1,0:T(8,128)(2,1)} %grads_ref.5, bf16[256,1024]{1,0:T(8,128)(2,1)} %acts_ref.5), custom_call_target="tpu_custom_call" | custom-call | tf_op jit(solution)/shard_map/project/pallas_call | solution.py:835
  370.6 4.5 %fusion = (f32[896,512]{1,0:T(8,128)S(1)}, f32[896,512]{1,0:T(8,128)}) fusion(f32[896,512]{1,0:T(8,128)} %get-tuple-element.10, f32[896,512]{1,0:T(8,128)} %param.11, f32[896,512]{1,0:T(8,128)} %param.10), kind=kLoop, calls=%fused_computation.2 | loop fusion | flops 3211264 | bytes 9175040 | tf_op jit(solution)/shard_map/add | solution.py:1006
  375.1 0.0 copy-start
  375.2 0.0 copy-start.1
  375.2 18.3 %convolution_multiply_fusion = f32[896,8192]{1,0:T(8,128)} fusion(bf16[8192,512]{1,0:T(8,128)(2,1)} %get-tuple-element.11, f32[896,512]{1,0:T(8,128)S(1)} %get-tuple-element.20, f32[896,512]{1,0:T(8,128)} %get-tuple-element.19), kind=kOutput, calls=%fused_computation | convolution fusion | flops 7525826560 | bytes 41418752 | tf_op jit(solution)/shard_map/dot_general | solution.py:33
  393.4 0.0 copy-done
  393.4 0.0 copy-done.1
  393.4 0.7 copy.11
Async XLA Ops:
  375.1 18.3 %copy-start = (f32[896,512]{1,0:T(8,128)}, f32[896,512]{1,0:T(8,128)S(1)}, u32[]{:S(2)}) copy-start(f32[896,512]{1,0:T(8,128)S(1)} %get-tuple-element.20) | copy-start | bytes 5505028
  375.2 18.3 %copy-start.1 = (bf16[256,512]{1,0:T(8,128)(2,1)S(1)}, bf16[256,512]{1,0:T(8,128)(2,1)}, u32[]{:S(2)}) copy-start(bf16[256,512]{1,0:T(8,128)(2,1)} %get-tuple-element.18.basis_ref) | copy-start | bytes 786436

commit v5 on v4

--- a/solution.py
+++ b/solution.py
@@ -26,6 +26,7 @@
 vmem_bytes = 63 * 2**20
 image_gather = 4
 image_ticks = (1, 0, 2, 2, 1, 1)
+power_group = 2
 power_lag, power_gap, power_ticks = 7, 4, (1, 3, 5, 7, 9, 11, 13, 15, 16)
 
 
@@ -319,7 +320,7 @@
 
 def power_kernel(
     rows, cols, acc, pair_ref, grads_ref, acts_ref, out_ref,
-    tiles, mine, theirs, pair_in, stage_in, chip_in,
+    tiles, held, pair_in, stage_in, chip_in,
     tile_sem, pair_sems, stage_sems, chip_sems, *reduce_scratch,
 ):
     g = Grid(rows, cols)
@@ -330,16 +331,26 @@
     half = g.count(0)
 
     def chip_of(w):
-        return g.chip(w, True)[0] if w < chips - 1 else g.z
+        if isinstance(w, int):
+            return g.chip(w, True)[0] if w < chips - 1 else g.z
+        far = g.z
+        for i, step in enumerate(g.offsets):
+            far = jnp.where(w == i, (g.z + step) % chips, far)
+        return far
+
+    mine = chips * rows
+
+    def core_of(kind):
+        return 1 - g.k + kind * (2 * g.k - 1)
 
     def block_of(t, kind=1):
         w, i = t // rows, t % rows
-        core = (1 - g.k) if kind == 0 else g.k
-        return w, g.block(0, i % half, g.peer_row(0, core) if i < half else g.r, core)
+        core = core_of(kind)
+        return w, g.block(0, i % half, jnp.where(i < half, g.peer_row(0, core), g.r), core)
 
     def fetch(t, kind):
         w, rp = block_of(t, kind)
-        core = (1 - g.k) if kind == 0 else g.k
+        core = core_of(kind)
         at = ((rp * chips + chip_of(w)) * 2 + core) * blk
         columns = pl.ds(pl.multiple_of(at, blk), blk)
         slot = kind * 2 + t % 2
@@ -357,48 +368,58 @@
 
     def pair_copy(w, rp):
         i = w * rows + rp
-        return remote(theirs.at[i], pair_in.at[i], pair_sems.at[0, i], pair_sems.at[1, i], g.partner)
+        return remote(held.at[i], pair_in.at[i], pair_sems.at[0, i], pair_sems.at[1, i], g.partner)
 
     def stage_copy(w, s, j):
         i = w * (rows - 1) + rows - 2 ** (stages - s) + j
-        source = mine.at[w * rows + g.block(s, j, g.peer_row(s))]
+        source = held.at[mine + w * rows + g.block(s, j, g.peer_row(s))]
         return remote(source, stage_in.at[i], stage_sems.at[0, i], stage_sems.at[1, i], g.peer(s))
 
     def chip_copy(w):
         return remote(
-            mine.at[w * rows + g.r], chip_in.at[w], chip_sems.at[0, w], chip_sems.at[1, w],
+            held.at[mine + w * rows + g.r], chip_in.at[w], chip_sems.at[0, w], chip_sems.at[1, w],
             g.chip_device(chip_of(w)),
         )
 
     def compute(t):
-        for kind, store in ((0, theirs), (1, mine)):
+        def one(kind, carry):
             w, rp = block_of(t, kind)
             fetch(t, kind).wait()
-            store[w * rows + rp] = product(kind * 2 + t % 2)
-            if kind == 0:
+            held[kind * mine + w * rows + rp] = product(kind * 2 + t % 2)
+
+            @pl.when(kind == 0)
+            def _():
                 pair_copy(w, rp).start()
-            if t + 2 < chips * rows:
+
+            @pl.when(t + 2 < chips * rows)
+            def _():
                 fetch(t + 2, kind).start()
+
+            return carry
+
+        lax.fori_loop(0, 2, one, 0)
 
     def pair(t):
         w, rp = block_of(t)
         pair_copy(w, rp).wait_recv()
-        mine[w * rows + rp] += pair_in[w * rows + rp]
-        if t % rows < half:
+        held[mine + w * rows + rp] += pair_in[w * rows + rp]
+
+        @pl.when(t % rows < half)
+        def _():
             stage_copy(w, 0, t % rows).start()
 
     def halve(w, s):
         for j in range(g.count(s - 1)):
             i = w * (rows - 1) + rows - 2 ** (stages - s + 1) + j
             stage_copy(w, s - 1, j).wait_recv()
-            mine[w * rows + g.block(s - 1, j, g.r)] += stage_in[i]
+            held[mine + w * rows + g.block(s - 1, j, g.r)] += stage_in[i]
         for j in range(g.count(s)):
             stage_copy(w, s, j).start()
 
     def leave(w):
         i = w * (rows - 1) + rows - 2
         stage_copy(w, stages - 1, 0).wait_recv()
-        mine[w * rows + g.r] += stage_in[i]
+        held[mine + w * rows + g.r] += stage_in[i]
         if w < chips - 1:
             chip_copy(w).start()
 
@@ -428,20 +449,30 @@
         later.setdefault(min(lag + gap * w + gap, steps + 2 * w + 3), []).append(
             functools.partial(leave, w)
         )
-    for t in range(max(max(later), steps) + 1):
-        if t in ticks:
+    def both(t, carry):
+        compute(t)
+
+        @pl.when(t > 0)
+        def _():
+            pair(t - 1)
+
+        return carry
+
+    for t in range(0, max(max(later), steps) + power_group, power_group):
+        for _ in range(sum(t <= at < t + power_group for at in ticks)):
             tick()
         if t < steps:
-            compute(t)
-        if 0 < t <= steps:
-            pair(t - 1)
-        for event in later.get(t, ()):
-            event()
+            lax.fori_loop(t, min(steps, t + power_group), both, 0)
+        if steps <= t < steps + power_group:
+            pair(steps - 1)
+        for at in range(t, t + power_group):
+            for event in later.get(at, ()):
+                event()
     for phase in phases:
         phase()
     upper, lower = split(full[...])
     total = mul(upper, acts_ref[...], cols_cols) + mul(lower, acts_ref[...], cols_cols)
-    total = total + mine[(chips - 1) * rows + g.r]
+    total = total + held[mine + (chips - 1) * rows + g.r]
     for w in range(chips - 1):
         chip_copy(w).wait_recv()
         total = total + chip_in[w]
@@ -474,8 +505,7 @@
         out_specs=VMEM,
         scratch_shapes=[
             pltpu.VMEM((4, accumulated.shape[0], blk), f32),
-            pltpu.VMEM((blocks, rank, blk), f32),
-            pltpu.VMEM((blocks, rank, blk), f32),
+            pltpu.VMEM((2 * blocks, rank, blk), f32),
             pltpu.VMEM((blocks, rank, blk), f32),
             pltpu.VMEM((passed, rank, blk), f32),
             pltpu.VMEM((chips - 1, rank, blk), f32),

time: 400 us -> 389 us (0.973); the launches traced: 395 us -> 388 us
  Pallas kernels: 370 us -> 364 us
    pallas_call x1, Pallas kernels: 111 us -> 107 us  [power_scatter(): pl.pallas_call(functools.partial(power_kernel, rows, cols), out_shape=jax...]
where the time goes in v5:
time: 389 us; the launch traced here: 388 us
  Pallas kernels  364 us (94%)
  matrix products  18.3 us (5%)
  other arithmetic  4.53 us (1%)
    pallas_call x1, Pallas kernels, power_scatter(): pl.pallas_call(functools.partial(power_kernel, rows, cols), out_shape=jax...  107 us
    pallas_call x1, Pallas kernels, image_pair(): pl.pallas_call(functools.partial(image_kernel, rows, cols), out_shape=jax...  103 us
    pallas_call x1, Pallas kernels, orthogonal(): pl.pallas_call(functools.partial(orthogonal_kernel, rows, cols, 128), out...  81.2 us
    pallas_call x1, Pallas kernels, project(): pl.pallas_call(functools.partial(project_kernel, rows, cols), out_shape=(...  73.9 us
    dot_general x1, matrix products, mul(): lax.dot_general(left, right, (dims, ((), ())), precision=precision, prefe...  18.3 us

profile of v5, /device:TPU:25, one launch (start us, length us, event | category | flops | bytes accessed | tf_op | source)
XLA Modules:
  0.0 388.5 jit_solution(4999486564500546207)
XLA Ops:
  0.6 102.7 %image_pair.1.pair_ref = bf16[1024,896]{1,0:T(8,128)(2,1)} custom-call(f32[896,8192]{1,0:T(8,128)} %acc.5, f32[2048,512]{1,0:T(8,128)} %seed_ref.1, bf16[896,1024]{1,0:T(8,128)(2,1)} %grads_ref.5, bf16[256,1024]{1,0:T(8,128)(2,1)} %acts_ref.5), custom_call_target="tpu_custom_call" | custom-call | tf_op jit(solution)/shard_map/image_pair/pallas_call | solution.py:723
  103.3 106.5 %power_scatter.1.power_ref = f32[512,256]{1,0:T(8,128)} custom-call(f32[896,8192]{1,0:T(8,128)} %acc.5, bf16[1024,896]{1,0:T(8,128)(2,1)} %image_pair.1.pair_ref, bf16[896,1024]{1,0:T(8,128)(2,1)} %grads_ref.5, bf16[256,1024]{1,0:T(8,128)(2,1)} %acts_ref.5), custom_call_target="tpu_custom_call" | custom-call | tf_op jit(solution)/shard_map/power_scatter/pallas_call | solution.py:501
  209.8 81.2 %orthogonal.1 = (bf16[256,512]{1,0:T(8,128)(2,1)}, bf16[512,256]{1,0:T(8,128)(2,1)}) custom-call(f32[512,256]{1,0:T(8,128)} %power_scatter.1.power_ref), custom_call_target="tpu_custom_call" | custom-call | tf_op jit(solution)/shard_map/orthogonal/pallas_call | solution.py:988
  291.1 73.9 %project.1 = (f32[896,512]{1,0:T(8,128)}, bf16[8192,512]{1,0:T(8,128)(2,1)}) custom-call(f32[896,8192]{1,0:T(8,128)} %acc.5, bf16[256,512]{1,0:T(8,128)(2,1)} %get-tuple-element.18.basis_ref, bf16[512,256]{1,0:T(8,128)(2,1)} %get-tuple-element.9.turned_ref, bf16[896,1024]{1,0:T(8,128)(2,1)} %grads_ref.5, bf16[256,1024]{1,0:T(8,128)(2,1)} %acts_ref.5), custom_call_target="tpu_custom_call" | custom-call | tf_op jit(solution)/shard_map/project/pallas_call | solution.py:865
  365.0 4.5 %fusion = (f32[896,512]{1,0:T(8,128)S(1)}, f32[896,512]{1,0:T(8,128)}) fusion(f32[896,512]{1,0:T(8,128)} %get-tuple-element.10, f32[896,512]{1,0:T(8,128)} %param.11, f32[896,512]{1,0:T(8,128)} %param.10), kind=kLoop, calls=%fused_computation.2 | loop fusion | flops 3211264 | bytes 9175040 | tf_op jit(solution)/shard_map/add | solution.py:1036
  369.5 0.0 copy-start
  369.5 0.0 copy-start.1
  369.5 18.3 %convolution_multiply_fusion = f32[896,8192]{1,0:T(8,128)} fusion(bf16[8192,512]{1,0:T(8,128)(2,1)} %get-tuple-element.11, f32[896,512]{1,0:T(8,128)S(1)} %get-tuple-element.20, f32[896,512]{1,0:T(8,128)} %get-tuple-element.19), kind=kOutput, calls=%fused_computation | convolution fusion | flops 7525826560 | bytes 41418752 | tf_op jit(solution)/shard_map/dot_general | solution.py:34
  387.8 0.0 copy-done
  387.8 0.0 copy-done.1
  387.8 0.7 copy.11
Async XLA Ops:
  369.5 18.3 %copy-start = (f32[896,512]{1,0:T(8,128)}, f32[896,512]{1,0:T(8,128)S(1)}, u32[]{:S(2)}) copy-start(f32[896,512]{1,0:T(8,128)S(1)} %get-tuple-element.20) | copy-start | bytes 5505028
  369.5 18.3 %copy-start.1 = (bf16[256,512]{1,0:T(8,128)(2,1)S(1)}, bf16[256,512]{1,0:T(8,128)(2,1)}, u32[]{:S(2)}) copy-start(bf16[256,512]{1,0:T(8,128)(2,1)} %get-tuple-element.18.basis_ref) | copy-start | bytes 786436

commit v6 on v5

--- a/solution.py
+++ b/solution.py
@@ -24,8 +24,9 @@
 VMEM = pl.BlockSpec(memory_space=pltpu.VMEM)
 DMA = pltpu.SemaphoreType.DMA
 vmem_bytes = 63 * 2**20
+project_ticks = (1, 1, 1, 1, 1, 1, 1)
 image_gather = 4
-image_ticks = (1, 0, 2, 2, 1, 1)
+image_ticks = (1, 0, 2, 1, 2, 1)
 power_group = 2
 power_lag, power_gap, power_ticks = 7, 4, (1, 3, 5, 7, 9, 11, 13, 15, 16)
 
@@ -221,75 +222,6 @@
     def drain(self):
         for copy in self.pending:
             copy.wait_send()
-
-
-class ChipsFirst(AllReduce):
-    def __init__(self, grid, *refs):
-        super().__init__(grid, *refs)
-        self.chunk = self.half // grid.chips
-        self.unit = self.chunk // grid.rows
-        self.phases = (
-            [self.pair_out, self.chips_out]
-            + [functools.partial(self.halve, s) for s in range(grid.stages)]
-            + [functools.partial(self.double, s) for s in reversed(range(grid.stages))]
-            + [self.chips_back, self.pair_back, self.finish]
-        )
-
-    @staticmethod
-    def scratch(rows, width, grid_rows, chips):
-        shapes = AllReduce.scratch(rows, width, grid_rows, chips)
-        half = rows // 2
-        unit = half // (chips * grid_rows)
-        shapes[3] = pltpu.VMEM((grid_rows - 1, unit, width), f32)
-        shapes[4] = pltpu.VMEM((chips - 1, half // chips, width), f32)
-        return shapes
-
-    def rows_of(self, r):
-        at = ((self.g.k * self.g.chips + self.g.z) * self.g.rows + r) * self.unit
-        return pl.ds(pl.multiple_of(at, self.unit), self.unit)
-
-    def chunk_of(self, z):
-        at = (self.g.k * self.g.chips + z) * self.chunk
-        return pl.ds(pl.multiple_of(at, self.chunk), self.chunk)
-
-    def chips_out(self):
-        g = self.g
-        self.landed()
-        mine = pl.ds(pl.multiple_of(g.k * self.half, self.half), self.half)
-        self.part[mine] += self.half_in[...]
-        for w in range(g.chips - 1):
-            z = g.chip(w)[0]
-            self.start(self.part.at[self.chunk_of(z)], self.chip_in.at[w], g.chip_device(z))
-
-    def halve(self, s):
-        g = self.g
-        self.landed()
-        if s == 0:
-            own = self.chunk_of(g.z)
-            total = self.part[own]
-            for w in range(g.chips - 1):
-                total = total + self.chip_in[w]
-            self.part[own] = total
-        else:
-            self.take(s - 1)
-        for j in range(g.count(s)):
-            rows = self.rows_of(g.block(s, j, g.peer_row(s)))
-            self.start(self.part.at[rows], self.stage_in.at[self.stage_base(s) + j], g.peer(s))
-
-    def double(self, s):
-        g = self.g
-        if s == g.stages - 1:
-            self.landed()
-            self.take(s)
-            self.full[self.rows_of(g.r)] = self.part[self.rows_of(g.r)]
-        super().double(s)
-
-    def chips_back(self):
-        g = self.g
-        self.landed()
-        own = self.chunk_of(g.z)
-        for w in range(g.chips - 1):
-            self.start(self.full.at[own], self.full.at[own], g.chip_device(g.chip(w)[0]))
 
 
 def reduce_kernel(rows, cols, part_ref, out_ref, *scratch):
@@ -661,7 +593,7 @@
     part, full, *rest = reduce_scratch
     upper, lower = split(turned)
     part[...] = mul(upper, acts_ref[...], rows_cols) + mul(lower, acts_ref[...], rows_cols)
-    tokens = ChipsFirst(g, part, full, *rest)
+    tokens = AllReduce(g, part, full, *rest)
     small = Interleaved(tokens.phases)
     small.tick()
 
@@ -733,7 +665,7 @@
             DMA((2, pieces * rows)),
             DMA((2, pieces * (rows - 1))),
             DMA((2, (cols // 2 - 1) * (rows - 1))),
-            *ChipsFirst.scratch(rank, acts.shape[1], rows, cols // 2),
+            *AllReduce.scratch(rank, acts.shape[1], rows, cols // 2),
         ],
         compiler_params=pltpu.CompilerParams(
             collective_id=collective_id, has_side_effects=True, vmem_limit_bytes=vmem_bytes
@@ -831,7 +763,7 @@
         return carry
 
     for at in range(chips + stages + 1):
-        small.tick()
+        small.tick(project_ticks[at] if at < len(project_ticks) else 1)
         for late in range(stages + 1):
             w = at - late
             if 0 <= w < chips:

time: 389 us -> 380 us (0.977)
  Pallas kernels: 364 us -> 355 us
    pallas_call x1, Pallas kernels: 103 us -> 91.3 us  [image_pair(): pl.pallas_call(functools.partial(image_kernel, rows, cols), out_shape=jax...]
where the time goes in v6:
time: 380 us; the launch traced here: 379 us
  Pallas kernels  355 us (93%)
  matrix products  18.3 us (5%)
  other arithmetic  4.53 us (1%)
    pallas_call x1, Pallas kernels, power_scatter(): pl.pallas_call(functools.partial(power_kernel, rows, cols), out_shape=jax...  109 us
    pallas_call x1, Pallas kernels, image_pair(): pl.pallas_call(functools.partial(image_kernel, rows, cols), out_shape=jax...  91.3 us
    pallas_call x1, Pallas kernels, orthogonal(): pl.pallas_call(functools.partial(orthogonal_kernel, rows, cols, 128), out...  80.9 us
    pallas_call x1, Pallas kernels, project(): pl.pallas_call(functools.partial(project_kernel, rows, cols), out_shape=(...  74.3 us
    dot_general x1, matrix products, mul(): lax.dot_general(left, right, (dims, ((), ())), precision=precision, prefe...  18.3 us

profile of v6, /device:TPU:25, one launch (start us, length us, event | category | flops | bytes accessed | tf_op | source)
XLA Modules:
  0.0 379.3 jit_solution(17285439212320208101)
XLA Ops:
  0.6 91.3 %image_pair.1.pair_ref = bf16[1024,896]{1,0:T(8,128)(2,1)} custom-call(f32[896,8192]{1,0:T(8,128)} %acc.5, f32[2048,512]{1,0:T(8,128)} %seed_ref.1, bf16[896,1024]{1,0:T(8,128)(2,1)} %grads_ref.5, bf16[256,1024]{1,0:T(8,128)(2,1)} %acts_ref.5), custom_call_target="tpu_custom_call" | custom-call | tf_op jit(solution)/shard_map/image_pair/pallas_call | solution.py:655
  92.0 108.6 %power_scatter.1.power_ref = f32[512,256]{1,0:T(8,128)} custom-call(f32[896,8192]{1,0:T(8,128)} %acc.5, bf16[1024,896]{1,0:T(8,128)(2,1)} %image_pair.1.pair_ref, bf16[896,1024]{1,0:T(8,128)(2,1)} %grads_ref.5, bf16[256,1024]{1,0:T(8,128)(2,1)} %acts_ref.5), custom_call_target="tpu_custom_call" | custom-call | tf_op jit(solution)/shard_map/power_scatter/pallas_call | solution.py:433
  200.6 80.9 %orthogonal.1 = (bf16[256,512]{1,0:T(8,128)(2,1)}, bf16[512,256]{1,0:T(8,128)(2,1)}) custom-call(f32[512,256]{1,0:T(8,128)} %power_scatter.1.power_ref), custom_call_target="tpu_custom_call" | custom-call | tf_op jit(solution)/shard_map/orthogonal/pallas_call | solution.py:920
  281.6 74.3 %project.1 = (f32[896,512]{1,0:T(8,128)}, bf16[8192,512]{1,0:T(8,128)(2,1)}) custom-call(f32[896,8192]{1,0:T(8,128)} %acc.5, bf16[256,512]{1,0:T(8,128)(2,1)} %get-tuple-element.18.basis_ref, bf16[512,256]{1,0:T(8,128)(2,1)} %get-tuple-element.9.turned_ref, bf16[896,1024]{1,0:T(8,128)(2,1)} %grads_ref.5, bf16[256,1024]{1,0:T(8,128)(2,1)} %acts_ref.5), custom_call_target="tpu_custom_call" | custom-call | tf_op jit(solution)/shard_map/project/pallas_call | solution.py:797
  355.8 4.5 %fusion = (f32[896,512]{1,0:T(8,128)S(1)}, f32[896,512]{1,0:T(8,128)}) fusion(f32[896,512]{1,0:T(8,128)} %get-tuple-element.10, f32[896,512]{1,0:T(8,128)} %param.11, f32[896,512]{1,0:T(8,128)} %param.10), kind=kLoop, calls=%fused_computation.2 | loop fusion | flops 3211264 | bytes 9175040 | tf_op jit(solution)/shard_map/add | solution.py:968
  360.4 0.0 copy-start
  360.4 0.0 copy-start.1
  360.4 18.3 %convolution_multiply_fusion = f32[896,8192]{1,0:T(8,128)} fusion(bf16[8192,512]{1,0:T(8,128)(2,1)} %get-tuple-element.11, f32[896,512]{1,0:T(8,128)S(1)} %get-tuple-element.20, f32[896,512]{1,0:T(8,128)} %get-tuple-element.19), kind=kOutput, calls=%fused_computation | convolution fusion | flops 7525826560 | bytes 41418752 | tf_op jit(solution)/shard_map/dot_general | solution.py:35
  378.6 0.0 copy-done
  378.6 0.0 copy-done.1
  378.6 0.7 copy.11
Async XLA Ops:
  360.4 18.3 %copy-start = (f32[896,512]{1,0:T(8,128)}, f32[896,512]{1,0:T(8,128)S(1)}, u32[]{:S(2)}) copy-start(f32[896,512]{1,0:T(8,128)S(1)} %get-tuple-element.20) | copy-start | bytes 5505028
  360.4 18.3 %copy-start.1 = (bf16[256,512]{1,0:T(8,128)(2,1)S(1)}, bf16[256,512]{1,0:T(8,128)(2,1)}, u32[]{:S(2)}) copy-start(bf16[256,512]{1,0:T(8,128)(2,1)} %get-tuple-element.18.basis_ref) | copy-start | bytes 786436

commit v7 on v6

--- a/solution.py
+++ b/solution.py
@@ -28,7 +28,7 @@
 image_gather = 4
 image_ticks = (1, 0, 2, 1, 2, 1)
 power_group = 2
-power_lag, power_gap, power_ticks = 7, 4, (1, 3, 5, 7, 9, 11, 13, 15, 16)
+power_lag, power_gap, power_ticks = 7, 4, (1, 5, 7, 9, 11, 13, 15, 17, 17)
 
 
 def mul(left, right, dims, precision=None):

time: 380 us -> 376 us (0.989)
  no operation moved by 1% of the time
where the time goes in v7:
time: 376 us
  Pallas kernels  352 us (94%)
  matrix products  18.3 us (5%)
  other arithmetic  4.53 us (1%)
    pallas_call x1, Pallas kernels, power_scatter(): pl.pallas_call(functools.partial(power_kernel, rows, cols), out_shape=jax...  106 us
    pallas_call x1, Pallas kernels, image_pair(): pl.pallas_call(functools.partial(image_kernel, rows, cols), out_shape=jax...  91.3 us
    pallas_call x1, Pallas kernels, orthogonal(): pl.pallas_call(functools.partial(orthogonal_kernel, rows, cols, 128), out...  81.4 us
    pallas_call x1, Pallas kernels, project(): pl.pallas_call(functools.partial(project_kernel, rows, cols), out_shape=(...  73 us
    dot_general x1, matrix products, mul(): lax.dot_general(left, right, (dims, ((), ())), precision=precision, prefe...  18.3 us

profile of v7, /device:TPU:25, one launch (start us, length us, event | category | flops | bytes accessed | tf_op | source)
XLA Modules:
  0.0 375.8 jit_solution(6708843791127006115)
XLA Ops:
  0.6 91.3 %image_pair.1.pair_ref = bf16[1024,896]{1,0:T(8,128)(2,1)} custom-call(f32[896,8192]{1,0:T(8,128)} %acc.5, f32[2048,512]{1,0:T(8,128)} %seed_ref.1, bf16[896,1024]{1,0:T(8,128)(2,1)} %grads_ref.5, bf16[256,1024]{1,0:T(8,128)(2,1)} %acts_ref.5), custom_call_target="tpu_custom_call" | custom-call | tf_op jit(solution)/shard_map/image_pair/pallas_call | solution.py:655
  92.0 105.8 %power_scatter.1.power_ref = f32[512,256]{1,0:T(8,128)} custom-call(f32[896,8192]{1,0:T(8,128)} %acc.5, bf16[1024,896]{1,0:T(8,128)(2,1)} %image_pair.1.pair_ref, bf16[896,1024]{1,0:T(8,128)(2,1)} %grads_ref.5, bf16[256,1024]{1,0:T(8,128)(2,1)} %acts_ref.5), custom_call_target="tpu_custom_call" | custom-call | tf_op jit(solution)/shard_map/power_scatter/pallas_call | solution.py:433
  197.8 81.4 %orthogonal.1 = (bf16[256,512]{1,0:T(8,128)(2,1)}, bf16[512,256]{1,0:T(8,128)(2,1)}) custom-call(f32[512,256]{1,0:T(8,128)} %power_scatter.1.power_ref), custom_call_target="tpu_custom_call" | custom-call | tf_op jit(solution)/shard_map/orthogonal/pallas_call | solution.py:920
  279.2 73.0 %project.1 = (f32[896,512]{1,0:T(8,128)}, bf16[8192,512]{1,0:T(8,128)(2,1)}) custom-call(f32[896,8192]{1,0:T(8,128)} %acc.5, bf16[256,512]{1,0:T(8,128)(2,1)} %get-tuple-element.18.basis_ref, bf16[512,256]{1,0:T(8,128)(2,1)} %get-tuple-element.9.turned_ref, bf16[896,1024]{1,0:T(8,128)(2,1)} %grads_ref.5, bf16[256,1024]{1,0:T(8,128)(2,1)} %acts_ref.5), custom_call_target="tpu_custom_call" | custom-call | tf_op jit(solution)/shard_map/project/pallas_call | solution.py:797
  352.2 4.5 %fusion = (f32[896,512]{1,0:T(8,128)S(1)}, f32[896,512]{1,0:T(8,128)}) fusion(f32[896,512]{1,0:T(8,128)} %get-tuple-element.10, f32[896,512]{1,0:T(8,128)} %param.11, f32[896,512]{1,0:T(8,128)} %param.10), kind=kLoop, calls=%fused_computation.2 | loop fusion | flops 3211264 | bytes 9175040 | tf_op jit(solution)/shard_map/add | solution.py:968
  356.8 0.0 copy-start
  356.8 0.0 copy-start.1
  356.8 18.3 %convolution_multiply_fusion = f32[896,8192]{1,0:T(8,128)} fusion(bf16[8192,512]{1,0:T(8,128)(2,1)} %get-tuple-element.11, f32[896,512]{1,0:T(8,128)S(1)} %get-tuple-element.20, f32[896,512]{1,0:T(8,128)} %get-tuple-element.19), kind=kOutput, calls=%fused_computation | convolution fusion | flops 7525826560 | bytes 41418752 | tf_op jit(solution)/shard_map/dot_general | solution.py:35
  375.1 0.0 copy-done
  375.1 0.0 copy-done.1
  375.1 0.7 copy.11
Async XLA Ops:
  356.8 18.3 %copy-start = (f32[896,512]{1,0:T(8,128)}, f32[896,512]{1,0:T(8,128)S(1)}, u32[]{:S(2)}) copy-start(f32[896,512]{1,0:T(8,128)S(1)} %get-tuple-element.20) | copy-start | bytes 5505028
  356.8 18.3 %copy-start.1 = (bf16[256,512]{1,0:T(8,128)(2,1)S(1)}, bf16[256,512]{1,0:T(8,128)(2,1)}, u32[]{:S(2)}) copy-start(bf16[256,512]{1,0:T(8,128)(2,1)} %get-tuple-element.18.basis_ref) | copy-start | bytes 786436
